TPU v7x, 512 devices: a whole 4x8x8 slice. The times are simulated.
512 devices in a mesh: pipe: 32 (over x, y), tensor: 16 (over z, core).
Axes of the slice: x: 4, y: 8, z: 8, core: 2. Of those that a mesh axis runs over, the one named last changes fastest.
Arguments:
- residual: bfloat16 [256, 8192], P(None, 'pipe'), may hold values from -22 to 22
- norm_gain: bfloat16 [8192], P('pipe'), may hold values from 0.099609375 to 1.8984375
- gate_codes: int32 [4096, 26624], P('pipe', 'tensor'), may hold values from 0 to 255
- gate_scales: bfloat16 [64, 26624], P('pipe', 'tensor'), may hold values from 0.0012130737 to 0.004852295
- up_codes: int32 [4096, 26624], P('pipe', 'tensor'), may hold values from 0 to 255
- up_scales: bfloat16 [64, 26624], P('pipe', 'tensor'), may hold values from 0.0012130737 to 0.004852295
- down_codes: int32 [13312, 8192], P('tensor', 'pipe'), may hold values from 0 to 255
- down_scales: bfloat16 [208, 8192], P('tensor', 'pipe'), may hold values from 0.0008544922 to 0.0034179688
- hidden_signs: int32 [26624], P('tensor'), may hold values from 0 to 1
Outputs:
- layer_out: bfloat16 [256, 8192], P(None, 'pipe')
All inputs are finite; a program needn't handle non-finite values.
Results may differ from a plain program's by a relative error of at most 0.0075.
Values may be sent and summed in bfloat16 or wider, within the bound.
No kernel may reach another device: no remote copies, remote signals or barrier semaphores. Data moves between devices by JAX's collectives and lax.ppermute only.
A program may use at most 64 MiB of HBM per device.

v0:
```python
import math

import jax
import jax.numpy as jnp
from jax import lax
from jax.sharding import Mesh
from jax.sharding import PartitionSpec as P

D = 8192
FACTOR = 128
PIPE = ("pipe_0", "pipe_1")


EPSILON = 1e-05


def summed_rows(shard, axes, dim):
    if not axes:
        return shard
    nearer = lax.psum_scatter(shard, axes[0], scatter_dimension=dim, tiled=True)
    return summed_rows(nearer, axes[1:], dim)


def laid_out(blocks, dim):
    blocks = jnp.moveaxis(blocks, 0, dim)
    dims = blocks.shape
    return blocks.reshape(*dims[:dim], dims[dim] * dims[dim + 1], *dims[dim + 2 :])


def copy_for_each(shard, axis):
    copies = jnp.broadcast_to(shard, (lax.axis_size(axis), *shard.shape))
    return lax.all_to_all(copies, axis, split_axis=0, concat_axis=0, tiled=True)


def gathered_copies(shard, axis, dim):
    return laid_out(copy_for_each(shard, axis), dim)


def total_of_pieces(shard, axis):
    blocks = lax.all_gather(shard, axis)
    return blocks.sum(axis=0)


def walsh(dimension):
    indices = jnp.arange(dimension, dtype=jnp.int32)
    common_bits = jnp.bitwise_and(indices[:, None], indices[None, :])
    parity = jnp.zeros((dimension, dimension), jnp.int32)
    for shift_by in range(max(dimension.bit_length() - 1, 1)):
        parity = parity + jnp.bitwise_and(jnp.right_shift(common_bits, shift_by), 1)
    return (1 - 2 * jnp.bitwise_and(parity, 1)).astype(jnp.float32)


def dequantize(codes, scales):
    group_rows = 2 * codes.shape[0] // scales.shape[0]
    low_codes = jnp.bitwise_and(codes, 15)
    high_codes = jnp.right_shift(codes, 4)
    stacked = jnp.stack([low_codes, high_codes], axis=1).reshape(2 * codes.shape[0], codes.shape[1])
    spread_scales = jnp.repeat(scales.astype(jnp.float32), group_rows, axis=0)
    return ((stacked - 8).astype(jnp.float32) * spread_scales).astype(jnp.bfloat16)


def gated(gate_sum, up_sum, square_total):
    inverse = lax.rsqrt(square_total / D + EPSILON)[:, None]
    return (jax.nn.silu(gate_sum * inverse) * (up_sum * inverse)).astype(jnp.bfloat16)


def rotate(activated, hidden_signs):
    tensor_count = lax.axis_size("tensor")
    rows_here = activated.shape[0]
    local_hidden = activated.shape[1]
    blocks = local_hidden // FACTOR
    norm_factor = 1.0 / math.sqrt(tensor_count * FACTOR)
    sign_values = (2 * hidden_signs - 1).astype(jnp.bfloat16)
    signed = (activated * sign_values[None, :]).reshape(rows_here, blocks, FACTOR)
    factor_table = walsh(FACTOR).astype(jnp.bfloat16)
    within = jnp.einsum("rbc,cd->rbd", signed, factor_table, preferred_element_type=jnp.float32)
    slice_width = FACTOR // tensor_count
    tensor_table = walsh(tensor_count)
    pieces = within.reshape(rows_here, blocks, tensor_count, slice_width).transpose(2, 0, 1, 3)
    across = jnp.einsum(
        "st,tkbw->skbw",
        tensor_table,
        lax.all_to_all(pieces, "tensor", split_axis=0, concat_axis=0, tiled=True),
        precision=lax.Precision.HIGHEST,
    )
    result = (across * norm_factor).astype(jnp.bfloat16)
    mixed = lax.all_to_all(result, "tensor", split_axis=0, concat_axis=0, tiled=True)
    return mixed.transpose(1, 2, 0, 3).reshape(rows_here, local_hidden)


def shards(
    residual,
    norm_gain,
    gate_codes,
    gate_scales,
    up_codes,
    up_scales,
    down_codes,
    down_scales,
    hidden_signs,
):
    gate_weight = dequantize(gate_codes, gate_scales)
    up_weight = dequantize(up_codes, up_scales)
    down_weight = dequantize(down_codes, down_scales)
    residual_wide = residual.astype(jnp.float32)
    scaled_in = (residual_wide * norm_gain.astype(jnp.float32)[None, :]).astype(jnp.bfloat16)
    square_sums = jnp.sum(residual_wide * residual_wide, axis=1)
    gate_part = jnp.dot(scaled_in, gate_weight, preferred_element_type=jnp.float32)
    up_part = jnp.dot(scaled_in, up_weight, preferred_element_type=jnp.float32)
    gate_sum, up_sum, square_total = (
        summed_rows(gate_part, PIPE, 0),
        summed_rows(up_part, PIPE, 0),
        summed_rows(square_sums, PIPE, 0),
    )
    share_act = gated(gate_sum, up_sum, square_total)
    rotated = gathered_copies(rotate(share_act, hidden_signs), PIPE, 0)
    partial_out = jnp.dot(rotated, down_weight, preferred_element_type=jnp.float32)
    total = total_of_pieces(partial_out, "tensor")
    return (residual_wide + total).astype(jnp.bfloat16)


def solution(mesh):
    torus = Mesh(mesh.devices.reshape(4, 8, mesh.shape["tensor"]), ("pipe_0", "pipe_1", "tensor"))
    placed = (
        P(None, PIPE),
        P(PIPE),
        P(PIPE, "tensor"),
        P(PIPE, "tensor"),
        P(PIPE, "tensor"),
        P(PIPE, "tensor"),
        P("tensor", PIPE),
        P("tensor", PIPE),
        P("tensor"),
    )
    return jax.shard_map(
        shards, mesh=torus, in_specs=placed, out_specs=P(None, PIPE), check_vma=False
    )
```

profile of v0, /device:TPU:1, one launch (start us, length us, event | category | flops | bytes accessed | tf_op | source)
XLA Modules:
  0.0 284.1 jit_solution(5847136011799039555)
XLA Ops:
  6.5 1.2 convert_element_type.100
  7.8 0.7 convert_element_type.104
  8.5 1.3 and_bitcast_fusion.2
  9.7 0.1 fusion
  9.8 1.3 copy.22
  11.2 1.2 convert_element_type.103
  12.4 0.0 copy-start.6
  12.4 0.1 fusion.4
  12.5 0.8 copy-done
  13.3 1.6 fusion.14
  14.9 0.0 reduce-scatter.3.cloned.1.call-update
  14.9 0.0 reduce-scatter.5.cloned.1.call-start
  15.0 0.1 and_bitcast_fusion.1
  15.1 0.1 fusion.1
  15.2 1.3 copy.23
  16.6 1.2 convert_element_type.107
  17.7 0.0 copy-start.7
  17.7 0.1 fusion.3
  17.9 0.6 copy-done.7
  18.4 1.6 fusion.12
  20.0 0.0 reduce-scatter.5.cloned.1.call-update
  20.0 0.0 all-reduce.7.cloned.1.call-start
  20.1 31.9 %reduce-scatter.3.cloned.1.call-done = f32[64,1664]{1,0:T(8,128)} async-done(((f32[256,1664]{1,0:T(8,128)}), f32[64,1664]{1,0:T(8,128)}) %reduce-scatter.3.cloned.1.call-update) | async-done | bytes 426000 | tf_op jit(solution)/shard_map/reduce_scatter | solution.py:20
  52.0 34.5 %reduce-scatter.5.cloned.1.call-done = f32[64,1664]{1,0:T(8,128)} async-done(((f32[256,1664]{1,0:T(8,128)}), f32[64,1664]{1,0:T(8,128)}) %reduce-scatter.5.cloned.1.call-update) | async-done | bytes 426000 | tf_op jit(solution)/shard_map/reduce_scatter | solution.py:20
  86.6 0.0 all-reduce.7.cloned.1.call-update
  86.6 1.3 dynamic-slice.2
  87.9 1.3 dynamic-slice
  89.2 0.1 and.168
  90.5 0.1 fusion.10
  90.6 6.8 %all-reduce.1 = f32[256]{0:T(256)S(1)} all-reduce(f32[256]{0:T(256)S(1)} %fusion.10), channel_id=5, replica_groups=mesh['pipe_0'=4,'pipe_1'=8,'tensor'=16] {'pipe_0'}, use_global_device_ids=true, to_apply=%region_3.0.clone | all-reduce | flops 256 | bytes 2048
  97.4 0.1 dynamic-slice.3
  97.5 13.9 %all-reduce.2 = f32[64]{0:T(128)S(1)} all-reduce(f32[64]{0:T(128)S(1)} %dynamic-slice.3), channel_id=6, replica_groups=mesh['pipe_0'=4,'pipe_1'=8,'tensor'=16] {'pipe_1'}, use_global_device_ids=true, to_apply=%region_4.0.clone | all-reduce | flops 64 | bytes 512
  111.4 0.1 fusion.46
  111.5 0.1 fusion.18
  111.6 53.2 %all-reduce.7.cloned.1.call-done = (f32[64,1664]{1,0:T(8,128)}, f32[64,1664]{1,0:T(8,128)}) async-done(((f32[64,1664]{1,0:T(8,128)}, f32[64,1664]{1,0:T(8,128)}), (f32[64,1664]{1,0:T(8,128)}, f32[64,1664]{1,0:T(8,128)})) %all-reduce.7.cloned.1.call-update) | async-done | bytes 851984
  164.8 0.9 multiply_bitcast_fusion
  165.7 0.2 convolution_bitcast_fusion
  165.9 0.6 copy.26
  166.6 0.4 reshape.92
  167.0 20.1 %all_to_all.15 = f32[16,1,832]{2,1,0:T(1,128)S(1)} all-to-all(f32[16,1,832]{2,1,0:T(1,128)S(1)} %reshape.92), channel_id=1, replica_groups=mesh['pipe_0'=4,'pipe_1'=8,'tensor'=16] {'tensor'}, dimensions={0} | all-to-all | bytes 106496 | tf_op jit(solution)/shard_map/all_to_all | solution.py:83
  187.1 0.5 broadcast.218
  187.6 0.8 reduce
  188.4 0.5 reshape.93
  188.9 0.8 fusion.5
  189.8 0.1 copy.44
  189.8 0.4 reshape.94
  190.2 10.1 %all_to_all.16 = bf16[16,2,416]{2,1,0:T(2,128)(2,1)S(1)} all-to-all(bf16[16,2,416]{2,1,0:T(2,128)(2,1)S(1)} %reshape.94), channel_id=1, replica_groups=mesh['pipe_0'=4,'pipe_1'=8,'tensor'=16] {'tensor'}, dimensions={0} | all-to-all | bytes 53248 | tf_op jit(solution)/shard_map/all_to_all | solution.py:87
  200.4 0.6 reshape.95
  201.0 1.0 copy.29
  202.0 0.4 reshape.82
  202.4 1.0 broadcast_in_dim.10
  203.4 6.8 %all-to-all-start.2 = ((bf16[32,8,1664]{2,1,0:T(8,128)(2,1)}), bf16[32,8,1664]{2,1,0:T(8,128)(2,1)}, u32[]{:S(2)}, u32[]{:S(2)}) async-start(bf16[32,8,1664]{2,1,0:T(8,128)(2,1)} %broadcast_in_dim.10), calls=%async_computation.4 | async-start | bytes 1703936 | tf_op jit(solution)/shard_map/all_to_all | solution.py:32
  210.3 0.0 all-gather.3.cloned.1.call-start
  210.3 0.1 and_bitcast_fusion
  210.5 0.1 fusion.2
  210.6 1.3 copy.30
  211.9 1.2 convert_element_type.117
  213.1 0.2 multiply_convert_fusion
  213.2 18.1 %all-to-all-done.2 = bf16[32,8,1664]{2,1,0:T(8,128)(2,1)} async-done(((bf16[32,8,1664]{2,1,0:T(8,128)(2,1)}), bf16[32,8,1664]{2,1,0:T(8,128)(2,1)}, u32[]{:S(2)}, u32[]{:S(2)}) %all-to-all-start.2) | async-done | bytes 852000 | tf_op jit(solution)/shard_map/all_to_all | solution.py:32
  231.3 2.3 fusion.6
  233.6 0.0 all-gather.3.cloned.1.call-update
  233.6 40.8 %all-gather.3.cloned.1.call-done = f32[4096,256]{1,0:T(8,128)} async-done(((f32[256,256]{1,0:T(8,128)}), f32[4096,256]{1,0:T(8,128)}) %all-gather.3.cloned.1.call-update) | async-done | bytes 4194320 | tf_op jit(solution)/shard_map/all_gather | solution.py:40
  274.4 2.5 reduce_sum.19
  276.9 0.7 fusion.11
  (18 shorter events, 0.1 us)
Async XLA Ops:
  6.5 45.5 %reduce-scatter.3.cloned.1.call-start = ((), (), s32[]{:S(2)}) async-start(), calls=%async_computation.5 | async-start | bytes 2129920 | tf_op jit(solution)/shard_map/reduce_scatter | solution.py:20
  12.3 0.9 copy-start
  12.4 0.9 copy-start.6
  13.3 1.7 copy-start.5
  13.3 1.7 copy-start.1
  14.9 71.7 %reduce-scatter.5.cloned.1.call-start = ((), (), s32[]{:S(2)}) async-start(), calls=%async_computation.6 | async-start | bytes 2129920 | tf_op jit(solution)/shard_map/reduce_scatter | solution.py:20
  17.7 0.7 copy-start.7
  20.0 91.5 %copy-start.4 = (s32[1664]{0:T(1024)S(1)}, s32[1664]{0:T(1024)}, u32[]{:S(2)}) copy-start(s32[1664]{0:T(1024)} %param.17) | copy-start | bytes 19972
  20.0 144.7 %all-reduce.7.cloned.1.call-start = ((), (), s32[]{:S(2)}) async-start(), calls=%async_computation.8 | async-start | bytes 1703936
  201.0 9.3 %copy-start.3 = (bf16[13,256]{1,0:T(8,128)(2,1)S(1)}, bf16[13,256]{1,0:T(8,128)(2,1)}, u32[]{:S(2)}) copy-start(bf16[13,256]{1,0:T(8,128)(2,1)} %param.16) | copy-start | bytes 19972
  201.0 9.3 %copy-start.2 = (s32[832,256]{1,0:T(8,128)S(1)}, s32[832,256]{1,0:T(8,128)}, u32[]{:S(2)}) copy-start(s32[832,256]{1,0:T(8,128)} %param.15) | copy-start | bytes 2555908
  203.4 27.9 %all-to-all-start.2 = ((bf16[32,8,1664]{2,1,0:T(8,128)(2,1)}), bf16[32,8,1664]{2,1,0:T(8,128)(2,1)}, u32[]{:S(2)}, u32[]{:S(2)}) async-start(bf16[32,8,1664]{2,1,0:T(8,128)(2,1)} %broadcast_in_dim.10), calls=%async_computation.4 | async-start | bytes 1703936 | tf_op jit(solution)/shard_map/all_to_all | solution.py:32
  210.3 64.1 %all-gather.3.cloned.1.call-start = ((), (), s32[]{:S(2)}) async-start(), calls=%async_computation.7 | async-start | bytes 4456448 | tf_op jit(solution)/shard_map/all_gather | solution.py:40
Sparse Core Ops, SparseCore 0:
  15.0 36.9 reduce-scatter.2
  54.9 31.6 reduce-scatter.4
  88.9 75.7 all-reduce.6
  233.7 40.6 all-gather.2
where the time goes:
time: 285 us; the launch traced here: 284 us
  waiting for transfers between devices  179 us (63%)
  blocking collectives  51 us (18%)
  local copies, waits for them, and re-layouts  17.1 us (6%)
  between operations  14.7 us (5%)
  other arithmetic  9.33 us (3%)
  starting transfers between devices  6.95 us (2%)
  matrix products  6.52 us (2%)
    reduce_scatter x2, waiting for transfers between devices, summed_rows(): nearer = lax.psum_scatter(shard, axes[0], scatter_dimension=dim, tiled=True)  66.5 us
    unnamed x5, waiting for transfers between devices  53.2 us
    all_gather x1, waiting for transfers between devices, total_of_pieces(): blocks = lax.all_gather(shard, axis)  40.8 us
    unnamed x2, blocking collectives  20.7 us
    all_to_all x1, blocking collectives, rotate(): lax.all_to_all(pieces, 'tensor', split_axis=0, concat_axis=0, tiled=True)  20.1 us
    all_to_all x1, waiting for transfers between devices, copy_for_each(): return lax.all_to_all(copies, axis, split_axis=0, concat_axis=0, tiled=True)  18.1 us
    all_to_all x1, blocking collectives, rotate(): lax.all_to_all(result, 'tensor', split_axis=0, concat_axis=0, tiled=True)  10.1 us
    convert_element_type x6, local copies, waits for them, and re-layouts, dequantize(): (stacked - 8).astype(jnp.float32) * spread_scales  7.46 us
  transfers between devices with their start and end apart: 5, of which 5 were waited for; matrix products, arithmetic and copies ran while one was open for 4% of the time, Pallas kernels for 0%

commit v1 on v0

v1 whole, which is shorter than its diff:
```python
import jax
import jax.numpy as jnp
from jax import lax
from jax.experimental import pallas as pl
from jax.experimental.pallas import tpu as pltpu
from jax.sharding import Mesh
from jax.sharding import PartitionSpec as P

D = 8192
ROWS = 256
FACTOR = 128
EPSILON = 1e-05
NEAR = ("x", "yl")
FAR = ("yh", "t")
N_NEAR = 8
N_YH = 4
N_T = 16
LOCAL = 1664
SLICE = LOCAL // N_T
BLOCKS = LOCAL // FACTOR
WIDE = 2 * LOCAL + 128
F32 = jnp.float32
BF16 = jnp.bfloat16


def parity_sign(common):
    parity = common
    for shift in (4, 2, 1):
        parity = parity ^ (parity >> shift)
    return (1 - 2 * (parity & 1)).astype(F32)


def call(body, out_shape, scratch=()):
    return pl.pallas_call(
        body,
        out_shape=out_shape,
        scratch_shapes=scratch,
        compiler_params=pltpu.CompilerParams(vmem_limit_bytes=48 << 20),
    )


def project_in(x_ref, gain_ref, gate_codes, gate_scales, up_codes, up_scales, signs, out_ref):
    width = x_ref.shape[1]
    half = width // 2
    wide = x_ref[...].astype(F32)
    scaled = (wide * gain_ref[...].astype(F32)).astype(BF16)
    source = lax.broadcasted_iota(jnp.int32, (width, width), 0)
    target = lax.broadcasted_iota(jnp.int32, (width, width), 1)
    wanted = jnp.where(target < half, 2 * target, 2 * (target - half) + 1)
    order = (source == wanted).astype(F32).astype(BF16)
    ordered = jnp.dot(scaled, order, preferred_element_type=F32).astype(BF16)
    words = gate_codes.shape[0]
    top = lax.broadcasted_iota(jnp.int32, (words, FACTOR), 0) < words // 2

    for codes, scales, base in ((gate_codes, gate_scales, 0), (up_codes, up_scales, LOCAL)):
        for block in range(BLOCKS):
            lanes = pl.ds(block * FACTOR, FACTOR)
            word = codes[:, lanes]
            scale = scales[:, lanes].astype(F32)
            if base:
                scale = scale * (2 * signs[:, lanes] - 1).astype(F32)
            spread = jnp.where(top, scale[0:1, :], scale[1:2, :])
            low = (((word & 15) - 8).astype(F32) * spread).astype(BF16)
            high = (((word >> 4) - 8).astype(F32) * spread).astype(BF16)
            weight = jnp.concatenate([low, high], axis=0)
            part = jnp.dot(ordered, weight, preferred_element_type=F32)
            out_ref[:, pl.ds(base + block * FACTOR, FACTOR)] = part.astype(BF16)

    squares = jnp.sum(wide * wide, axis=1, keepdims=True)
    out_ref[:, pl.ds(2 * LOCAL, 128)] = two_parts(squares, ROWS)


def two_parts(value, rows):
    lane = lax.broadcasted_iota(jnp.int32, (rows, 128), 1)
    coarse = value.astype(BF16).astype(F32)
    fine = value - coarse
    return jnp.where(lane == 0, coarse, jnp.where(lane == 1, fine, 0.0)).astype(BF16)


def rotate_down(codes, scales, out_ref):
    row = lax.broadcasted_iota(jnp.int32, (FACTOR, FACTOR), 0)
    column = lax.broadcasted_iota(jnp.int32, (FACTOR, FACTOR), 1)
    half = FACTOR // 2
    column = jnp.where(column < half, 2 * column, 2 * (column - half) + 1)
    table = parity_sign(row & column).astype(BF16)
    norm = (N_T * FACTOR) ** -0.5
    for block in range(BLOCKS):
        word = codes[pl.ds(block * half, half), :]
        scale = scales[pl.ds(block, 1), :].astype(F32)
        low = (((word & 15) - 8).astype(F32) * scale).astype(BF16)
        high = (((word >> 4) - 8).astype(F32) * scale).astype(BF16)
        weight = jnp.concatenate([low, high], axis=0)
        mixed = jnp.dot(table, weight, preferred_element_type=F32) * norm
        out_ref[pl.ds(block * FACTOR, FACTOR), :] = mixed.astype(BF16)


def sum_near(parts, out_ref, total):
    rows = parts.shape[1]
    for block in range(WIDE // 128):
        lanes = pl.ds(block * 128, 128)
        value = parts[0, :, lanes].astype(F32)
        for source in range(1, N_NEAR):
            value = value + parts[source, :, lanes].astype(F32)
        total[:, lanes] = value
    squares = total[:, pl.ds(2 * LOCAL, 1)] + total[:, pl.ds(2 * LOCAL + 1, 1)]
    coarse = squares.astype(BF16).astype(F32)
    fine = squares - coarse
    lane = lax.broadcasted_iota(jnp.int32, (rows, 128), 1)
    for piece in range(N_T):
        gate = total[:, piece * SLICE : piece * SLICE + 128]
        gate = jnp.where(lane == SLICE, coarse, jnp.where(lane == SLICE + 1, fine, gate)).astype(BF16)
        up = total[:, LOCAL + piece * SLICE : LOCAL + piece * SLICE + 128].astype(BF16)
        for yh in range(N_YH):
            out_ref[yh * N_T + piece, :, 0:128] = gate[8 * yh : 8 * yh + 8, :]
            out_ref[yh * N_T + piece, :, 128:256] = up[8 * yh : 8 * yh + 8, :]


def activate(parts, out_ref):
    def summed(t):
        value = parts[t].astype(F32)
        for yh in range(1, N_YH):
            value = value + parts[yh * N_T + t].astype(F32)
        return value

    first = summed(0)
    squares = first[:, SLICE : SLICE + 1] + first[:, SLICE + 1 : SLICE + 2]
    inverse = lax.rsqrt(squares / D + EPSILON)
    values = []
    for t in range(N_T):
        both = first if t == 0 else summed(t)
        gate = both[:, 0:128] * inverse
        up = both[:, 128:256] * inverse
        act = gate / (1.0 + jnp.exp(-gate)) * up
        values.append(act.astype(BF16).astype(F32))
    step = 1
    while step < N_T:
        values = [
            values[i] + values[i + step] if not i & step else values[i - step] - values[i]
            for i in range(N_T)
        ]
        step *= 2
    for t in range(N_T):
        mixed = values[t].astype(BF16)
        for yh in range(N_YH):
            out_ref[yh * N_T + t] = mixed


def spread_near(parts, out_ref, joined):
    for piece in range(N_T):
        for yh in range(N_YH):
            joined[8 * yh : 8 * yh + 8, piece * SLICE : piece * SLICE + 128] = parts[yh * N_T + piece].astype(F32)
    for block in range(BLOCKS):
        lanes = pl.ds(block * 128, 128)
        value = joined[:, lanes].astype(BF16)
        for target in range(N_NEAR):
            out_ref[target, :, lanes] = value


def project_out(act, weight, out_ref):
    out_ref[...] = jnp.dot(act[...], weight[...], preferred_element_type=F32).astype(BF16)


def finish(here, parts, residual, out_ref):
    rows = ROWS // N_T
    value = parts[0].astype(F32)
    for t in range(1, N_T):
        value = value + parts[t].astype(F32)
    start = pl.multiple_of(here[0] * rows, rows)
    value = (value + residual[pl.ds(start, rows), :].astype(F32)).astype(BF16)
    for t in range(N_T):
        out_ref[t] = value


def exchange(blocks, axes):
    return lax.all_to_all(blocks, axes, split_axis=0, concat_axis=0, tiled=True)


def shards(residual, norm_gain, gate_codes, gate_scales, up_codes, up_scales, down_codes, down_scales, hidden_signs):
    shape = jax.ShapeDtypeStruct
    columns = residual.shape[1]
    part = call(project_in, shape((ROWS, WIDE), BF16))(
        residual, norm_gain[None, :], gate_codes, gate_scales, up_codes, up_scales, hidden_signs[None, :]
    )
    near_rows = ROWS // N_NEAR
    near = exchange(part.reshape(N_NEAR, near_rows, WIDE), NEAR)
    down_weight = call(rotate_down, shape((LOCAL, columns), BF16))(down_codes, down_scales)
    pieces = call(sum_near, shape((N_YH * N_T, 8, 256), BF16), [pltpu.VMEM((near_rows, WIDE), F32)])(near)
    far = exchange(pieces, FAR)
    mixed = call(activate, shape((N_YH * N_T, 8, 128), BF16))(far)
    back = exchange(mixed, FAR)
    copies = call(spread_near, shape((N_NEAR, near_rows, LOCAL), BF16), [pltpu.VMEM((near_rows, LOCAL + 128), F32)])(back)
    rotated = exchange(copies, NEAR).reshape(ROWS, LOCAL)
    partial = call(project_out, shape((ROWS, columns), BF16))(rotated, down_weight)
    sums = exchange(partial.reshape(N_T, ROWS // N_T, columns), "t")
    here = lax.axis_index("t").astype(jnp.int32).reshape(1)
    out = pl.pallas_call(
        finish,
        out_shape=shape((N_T, ROWS // N_T, columns), BF16),
        in_specs=[
            pl.BlockSpec(memory_space=pltpu.SMEM),
            pl.BlockSpec(memory_space=pltpu.VMEM),
            pl.BlockSpec(memory_space=pltpu.VMEM),
        ],
    )(here, sums, residual)
    return exchange(out, "t").reshape(ROWS, columns)


def solution(mesh):
    torus = Mesh(mesh.devices.reshape(4, N_YH, 2, N_T), ("x", "yh", "yl", "t"))
    pipe = ("x", "yh", "yl")
    placed = (
        P(None, pipe),
        P(pipe),
        P(pipe, "t"),
        P(pipe, "t"),
        P(pipe, "t"),
        P(pipe, "t"),
        P("t", pipe),
        P("t", pipe),
        P("t"),
    )
    return jax.shard_map(shards, mesh=torus, in_specs=placed, out_specs=P(None, pipe), check_vma=False)
```

time: 285 us -> 134 us (0.47)
  waiting for transfers between devices: 179 us -> 21.9 us
  blocking collectives: 51 us -> 89.8 us
  between operations: 14.7 us -> 0.06 us
  local copies, waits for them, and re-layouts: 17.1 us -> 7.28 us
  other arithmetic: 9.33 us -> 0 us
  matrix products: 6.52 us -> 0 us
  Pallas kernels: 0 us -> 6.17 us
    reduce_scatter x2 -> x0, waiting for transfers between devices: 66.5 us -> none  [summed_rows(): nearer = lax.psum_scatter(shard, axes[0], scatter_dimension=dim, tiled=True)]
    all_to_all x2 -> x4, blocking collectives: 30.3 us -> 89.8 us  [exchange(): return lax.all_to_all(blocks, axes, split_axis=0, concat_axis=0, tiled=True)]
    unnamed x5 -> x0, waiting for transfers between devices: 53.2 us -> none
    all_gather x1 -> x0, waiting for transfers between devices: 40.8 us -> none  [total_of_pieces(): blocks = lax.all_gather(shard, axis)]
    unnamed x2 -> x0, blocking collectives: 20.7 us -> none
    convert_element_type x7 -> x0, local copies, waits for them, and re-layouts: 7.53 us -> none  [the longest x6 7.46 us: dequantize(): (stacked - 8).astype(jnp.float32) * spread_scales]
    dot_general x5 -> x0, matrix products: 6.52 us -> none  [the longest x1 2.26 us: shards(): jnp.dot(rotated, down_weight, preferred_element_type=jnp.float32)]
    pallas_call x0 -> x7, Pallas kernels: none -> 6.17 us  [the longest x1 1.63 us: shards(): pl.pallas_call(finish, out_shape=shape((N_T, ROWS // N_T, columns), BF16)...]
  transfers between devices with their start and end apart: 5 -> 2, of which waited for: 5 -> 2; matrix products, arithmetic and copies ran while one was open for 4% -> 0% of each run, Pallas kernels for 0% -> 0%
where the time goes in v1:
time: 134 us; the launch traced here: 133 us
  blocking collectives  89.8 us (67%)
  waiting for transfers between devices  21.9 us (16%)
  starting transfers between devices  8.11 us (6%)
  local copies, waits for them, and re-layouts  7.28 us (5%)
  Pallas kernels  6.17 us (5%)
    all_to_all x4, blocking collectives, exchange(): return lax.all_to_all(blocks, axes, split_axis=0, concat_axis=0, tiled=True)  89.8 us
    all_to_all x2, waiting for transfers between devices, exchange(): return lax.all_to_all(blocks, axes, split_axis=0, concat_axis=0, tiled=True)  21.9 us
    all_to_all x2, starting transfers between devices, exchange(): return lax.all_to_all(blocks, axes, split_axis=0, concat_axis=0, tiled=True)  8.11 us
    unnamed x17, local copies, waits for them, and re-layouts  5.92 us
  transfers between devices with their start and end apart: 2, of which 2 were waited for; matrix products, arithmetic and copies ran while one was open for 0% of the time, Pallas kernels for 0%

profile of v1, /device:TPU:1, one launch (start us, length us, event | category | flops | bytes accessed | tf_op | source)
XLA Modules:
  0.0 133.3 jit_solution(722907799492487973)
XLA Ops:
  0.0 0.7 broadcast_in_dim.7.signs
  0.7 0.7 broadcast_in_dim.6.gain_ref
  1.4 0.0 copy-start
  1.4 1.2 copy-done
  2.5 0.0 copy-start.1
  2.5 1.2 copy-done.1
  3.7 0.0 copy-start.3
  3.7 0.9 copy-done.3
  4.6 0.0 copy-start.5
  4.6 0.7 copy-done.5
  5.3 0.0 copy-start.6
  5.3 0.7 copy-done.6
  6.0 1.3 shard_map.91
  7.2 25.7 %all_to_all.30.parts = bf16[8,32,3456]{2,1,0:T(8,128)(2,1)S(1)} all-to-all(bf16[8,32,3456]{2,1,0:T(8,128)(2,1)S(1)} %bitcast.5), channel_id=1, replica_groups=mesh['x'=4,'yh'=4,'yl'=2,'t'=16] {'x','yl'}, dimensions={0} | all-to-all | bytes 3538944 | tf_op jit(solution)/shard_map/all_to_all | solution.py:175
  33.0 0.3 shard_map.92
  33.3 33.5 %all_to_all.31.parts = bf16[64,8,256]{2,1,0:T(8,128)(2,1)S(1)} all-to-all(bf16[64,8,256]{2,1,0:T(8,128)(2,1)S(1)} %shard_map.92), channel_id=1, replica_groups=mesh['x'=4,'yh'=4,'yl'=2,'t'=16] {'yh','t'}, dimensions={0} | all-to-all | bytes 524288 | tf_op jit(solution)/shard_map/all_to_all | solution.py:175
  66.8 0.0 copy-start.2
  66.8 0.0 copy-start.4
  66.8 0.2 shard_map.93
  67.0 18.7 %all_to_all.32.parts = bf16[64,8,128]{2,1,0:T(8,128)(2,1)S(1)} all-to-all(bf16[64,8,128]{2,1,0:T(8,128)(2,1)S(1)} %shard_map.93), channel_id=1, replica_groups=mesh['x'=4,'yh'=4,'yl'=2,'t'=16] {'yh','t'}, dimensions={0} | all-to-all | bytes 262144 | tf_op jit(solution)/shard_map/all_to_all | solution.py:175
  85.8 1.2 shard_map.94
  86.9 3.5 %all-to-all-start.3 = ((bf16[8,32,1664]{2,1,0:T(8,128)(2,1)}), bf16[8,32,1664]{2,1,0:T(8,128)(2,1)S(1)}, u32[]{:S(2)}, u32[]{:S(2)}) async-start(bf16[8,32,1664]{2,1,0:T(8,128)(2,1)} %shard_map.94), calls=%async_computation.3 | async-start | bytes 1703936 | tf_op jit(solution)/shard_map/all_to_all | solution.py:175
  90.5 0.0 copy-done.2
  90.5 0.0 copy-done.4
  90.5 0.5 shard_map.95.weight
  91.0 12.7 %all-to-all-done.3 = bf16[8,32,1664]{2,1,0:T(8,128)(2,1)S(1)} async-done(((bf16[8,32,1664]{2,1,0:T(8,128)(2,1)}), bf16[8,32,1664]{2,1,0:T(8,128)(2,1)S(1)}, u32[]{:S(2)}, u32[]{:S(2)}) %all-to-all-start.3) | async-done | bytes 852000 | tf_op jit(solution)/shard_map/all_to_all | solution.py:175
  103.7 1.1 shard_map.96
  104.8 4.6 %all-to-all-start.4 = ((bf16[16,16,256]{2,1,0:T(8,128)(2,1)}), bf16[16,16,256]{2,1,0:T(8,128)(2,1)S(1)}, u32[]{:S(2)}, u32[]{:S(2)}) async-start(bf16[16,16,256]{2,1,0:T(8,128)(2,1)} %bitcast.3), calls=%async_computation.4 | async-start | bytes 262144 | tf_op jit(solution)/shard_map/all_to_all | solution.py:175
  109.4 9.2 %all-to-all-done.4.parts = bf16[16,16,256]{2,1,0:T(8,128)(2,1)S(1)} async-done(((bf16[16,16,256]{2,1,0:T(8,128)(2,1)}), bf16[16,16,256]{2,1,0:T(8,128)(2,1)S(1)}, u32[]{:S(2)}, u32[]{:S(2)}) %all-to-all-start.4) | async-done | bytes 131104 | tf_op jit(solution)/shard_map/all_to_all | solution.py:175
  118.5 0.0 copy-start.7
  118.5 0.7 copy-done.7
  119.2 1.6 %shard_map.97 = bf16[16,16,256]{2,1,0:T(8,128)(2,1)} custom-call(s32[1]{0:T(128)} %bitcast.here, bf16[16,16,256]{2,1,0:T(8,128)(2,1)} %copy-done.7, bf16[256,256]{1,0:T(8,128)(2,1)} %residual.1), custom_call_target="tpu_custom_call" | custom-call | tf_op jit(solution)/shard_map/pallas_call | solution.py:196
  120.8 11.8 %all_to_all.33 = bf16[16,16,256]{2,1,0:T(8,128)(2,1)S(1)} all-to-all(bf16[16,16,256]{2,1,0:T(8,128)(2,1)} %shard_map.97), channel_id=1, replica_groups=mesh['x'=4,'yh'=4,'yl'=2,'t'=16] {'t'}, dimensions={0} | all-to-all | bytes 262144 | tf_op jit(solution)/shard_map/all_to_all | solution.py:175
  132.7 0.7 copy.11
Async XLA Ops:
  1.4 1.2 copy-start
  2.5 1.2 copy-start.1
  3.7 0.9 copy-start.3
  4.6 0.7 copy-start.5
  5.3 0.7 copy-start.6
  66.8 23.7 %copy-start.2 = (s32[832,256]{1,0:T(8,128)S(1)}, s32[832,256]{1,0:T(8,128)}, u32[]{:S(2)}) copy-start(s32[832,256]{1,0:T(8,128)} %codes.1) | copy-start | bytes 2555908
  66.8 23.7 %copy-start.4 = (bf16[13,256]{1,0:T(8,128)(2,1)S(1)}, bf16[13,256]{1,0:T(8,128)(2,1)}, u32[]{:S(2)}) copy-start(bf16[13,256]{1,0:T(8,128)(2,1)} %scales.1) | copy-start | bytes 19972
  86.9 16.8 %all-to-all-start.3 = ((bf16[8,32,1664]{2,1,0:T(8,128)(2,1)}), bf16[8,32,1664]{2,1,0:T(8,128)(2,1)S(1)}, u32[]{:S(2)}, u32[]{:S(2)}) async-start(bf16[8,32,1664]{2,1,0:T(8,128)(2,1)} %shard_map.94), calls=%async_computation.3 | async-start | bytes 1703936 | tf_op jit(solution)/shard_map/all_to_all | solution.py:175
  104.8 13.7 %all-to-all-start.4 = ((bf16[16,16,256]{2,1,0:T(8,128)(2,1)}), bf16[16,16,256]{2,1,0:T(8,128)(2,1)S(1)}, u32[]{:S(2)}, u32[]{:S(2)}) async-start(bf16[16,16,256]{2,1,0:T(8,128)(2,1)} %bitcast.3), calls=%async_computation.4 | async-start | bytes 262144 | tf_op jit(solution)/shard_map/all_to_all | solution.py:175
  118.5 0.7 copy-start.7

commit v2 on v1

v2 whole, which is shorter than its diff:
```python
import jax
import jax.numpy as jnp
from jax import lax
from jax.experimental import pallas as pl
from jax.experimental.pallas import tpu as pltpu
from jax.sharding import Mesh
from jax.sharding import PartitionSpec as P

D = 8192
ROWS = 256
FACTOR = 128
EPSILON = 1e-05
NEAR = ("x", "yl")
FAR = ("yh", "zh")
TENSOR = ("zh", "zl", "c")
N_NEAR = 8
N_YH = 4
N_ZH = 4
N_T = 16
LOCAL = 1664
SLICE = LOCAL // N_ZH
BLOCKS = LOCAL // FACTOR
WIDE = 2 * LOCAL + 128
PIECE = 2 * SLICE + 64
NEAR_ROWS = ROWS // N_NEAR
OWN_ROWS = ROWS // N_T
F32 = jnp.float32
BF16 = jnp.bfloat16


def parity_sign(common):
    parity = common
    for shift in (4, 2, 1):
        parity = parity ^ (parity >> shift)
    return (1 - 2 * (parity & 1)).astype(F32)


def call(body, out_shape, scratch=()):
    return pl.pallas_call(
        body,
        out_shape=out_shape,
        scratch_shapes=scratch,
        compiler_params=pltpu.CompilerParams(vmem_limit_bytes=48 << 20),
    )


def two_parts(value, lanes):
    lane = lax.broadcasted_iota(jnp.int32, (value.shape[0], lanes), 1)
    coarse = value.astype(BF16).astype(F32)
    return jnp.where(lane == 0, coarse, jnp.where(lane == 1, value - coarse, 0.0))


def project_in(x_hbm, gain_hbm, gate_hbm, gate_scales_hbm, up_hbm, up_scales_hbm, signs_hbm, out_ref, own_ref, *scratch):
    x_ref, gain_ref, gate_codes, gate_scales, up_codes, up_scales, signs, sems = scratch
    small = [
        pltpu.make_async_copy(source, target, sems.at[i])
        for i, (source, target) in enumerate(
            [(x_hbm, x_ref), (gain_hbm, gain_ref), (gate_scales_hbm, gate_scales), (up_scales_hbm, up_scales), (signs_hbm, signs)]
        )
    ]
    for copy in small:
        copy.start()
    copies = {}
    starts = (0, 4, 7, 10, BLOCKS)
    slot = len(small)
    for which, (source, target) in enumerate(((gate_hbm, gate_codes), (up_hbm, up_codes))):
        for first, last in zip(starts[:-1], starts[1:]):
            lanes = pl.ds(first * FACTOR, (last - first) * FACTOR)
            copies[which, first] = pltpu.make_async_copy(source.at[:, lanes], target.at[:, lanes], sems.at[slot])
            copies[which, first].start()
            slot += 1

    width = x_ref.shape[1]
    half = width // 2
    source = lax.broadcasted_iota(jnp.int32, (width, width), 0)
    target = lax.broadcasted_iota(jnp.int32, (width, width), 1)
    wanted = jnp.where(target < half, 2 * target, 2 * (target - half) + 1)
    order = (source == wanted).astype(F32).astype(BF16)
    words = gate_codes.shape[0]
    top = lax.broadcasted_iota(jnp.int32, (words, FACTOR), 0) < words // 2
    my_t = (lax.axis_index("zh") * 2 + lax.axis_index("zl")) * 2 + lax.axis_index("c")
    for copy in small:
        copy.wait()
    wide = x_ref[...].astype(F32)
    scaled = (wide * gain_ref[...].reshape(1, width).astype(F32)).astype(BF16)
    ordered = jnp.dot(scaled, order, preferred_element_type=F32).astype(BF16)
    squares = jnp.sum(wide * wide, axis=1, keepdims=True)
    out_ref[:, pl.ds(2 * LOCAL, 128)] = two_parts(squares, 128).astype(BF16)
    own_ref[...] = x_ref[pl.ds(pl.multiple_of(my_t * OWN_ROWS, OWN_ROWS), OWN_ROWS), :]

    for which, (codes, scales, base) in enumerate(((gate_codes, gate_scales, 0), (up_codes, up_scales, LOCAL))):
        for block in range(BLOCKS):
            if (which, block) in copies:
                copies[which, block].wait()
            lanes = pl.ds(block * FACTOR, FACTOR)
            word = codes[:, lanes]
            scale = scales[:, lanes].astype(F32)
            if base:
                scale = scale * (2 * signs[lanes].reshape(1, FACTOR) - 1).astype(F32)
            spread = jnp.where(top, scale[0:1, :], scale[1:2, :])
            low = (((word & 15) - 8).astype(F32) * spread).astype(BF16)
            high = (((word >> 4) - 8).astype(F32) * spread).astype(BF16)
            weight = jnp.concatenate([low, high], axis=0)
            part = jnp.dot(ordered, weight, preferred_element_type=F32)
            out_ref[:, pl.ds(base + block * FACTOR, FACTOR)] = part.astype(BF16)


def rotate_down(codes, scales, out_ref):
    row = lax.broadcasted_iota(jnp.int32, (FACTOR, FACTOR), 0)
    column = lax.broadcasted_iota(jnp.int32, (FACTOR, FACTOR), 1)
    half = FACTOR // 2
    column = jnp.where(column < half, 2 * column, 2 * (column - half) + 1)
    table = parity_sign(row & column).astype(BF16)
    norm = (N_T * FACTOR) ** -0.5
    for block in range(BLOCKS):
        word = codes[pl.ds(block * half, half), :]
        scale = scales[pl.ds(block, 1), :].astype(F32)
        low = (((word & 15) - 8).astype(F32) * scale).astype(BF16)
        high = (((word >> 4) - 8).astype(F32) * scale).astype(BF16)
        weight = jnp.concatenate([low, high], axis=0)
        mixed = jnp.dot(table, weight, preferred_element_type=F32) * norm
        out_ref[pl.ds(block * FACTOR, FACTOR), :] = mixed.astype(BF16)


def sum_near(parts, out_ref, total, joined):
    for block in range(WIDE // 128):
        lanes = pl.ds(block * 128, 128)
        value = parts[0, :, lanes].astype(F32)
        for source in range(1, N_NEAR):
            value = value + parts[source, :, lanes].astype(F32)
        total[:, lanes] = value
    squares = total[:, pl.ds(2 * LOCAL, 1)] + total[:, pl.ds(2 * LOCAL + 1, 1)]
    tail = two_parts(squares, 64)
    for piece in range(N_ZH):
        joined[:, 0:SLICE] = total[:, piece * SLICE : (piece + 1) * SLICE]
        joined[:, SLICE : 2 * SLICE] = total[:, LOCAL + piece * SLICE : LOCAL + (piece + 1) * SLICE]
        joined[:, 2 * SLICE : PIECE] = tail
        value = joined[...].astype(BF16)
        for yh in range(N_YH):
            out_ref[yh * N_ZH + piece] = value[8 * yh : 8 * yh + 8, :]


def activate(parts, out_ref, joined):
    values = []
    inverse = None
    for z in range(N_ZH):
        value = parts[z].astype(F32)
        for yh in range(1, N_YH):
            value = value + parts[yh * N_ZH + z].astype(F32)
        joined[...] = value
        if z == 0:
            squares = joined[:, 2 * SLICE : 2 * SLICE + 1] + joined[:, 2 * SLICE + 1 : 2 * SLICE + 2]
            inverse = lax.rsqrt(squares / D + EPSILON)
        gate = joined[:, 0:SLICE] * inverse
        up = joined[:, SLICE : 2 * SLICE] * inverse
        act = gate / (1.0 + jnp.exp(-gate)) * up
        values.append(act.astype(BF16).astype(F32))
    step = 1
    while step < N_ZH:
        values = [
            values[i] + values[i + step] if not i & step else values[i - step] - values[i]
            for i in range(N_ZH)
        ]
        step *= 2
    for z in range(N_ZH):
        mixed = values[z].astype(BF16)
        for yh in range(N_YH):
            out_ref[yh * N_ZH + z] = mixed


def spread_near(parts, out_ref, joined):
    for piece in range(N_ZH):
        for yh in range(N_YH):
            joined[8 * yh : 8 * yh + 8, piece * SLICE : (piece + 1) * SLICE] = parts[yh * N_ZH + piece].astype(F32)
    for block in range(BLOCKS):
        lanes = pl.ds(block * 128, 128)
        value = joined[:, lanes].astype(BF16)
        for target in range(N_NEAR):
            out_ref[target, :, lanes] = value


def project_out(act, weight, out_ref):
    out_ref[...] = jnp.dot(act[...], weight[...], preferred_element_type=F32).astype(BF16)


def finish(parts, residual, out_ref):
    value = residual[...].astype(F32)
    for t in range(N_T):
        value = value + parts[t].astype(F32)
    value = value.astype(BF16)
    for t in range(N_T):
        out_ref[t] = value


def exchange(blocks, axes):
    return lax.all_to_all(blocks, axes, split_axis=0, concat_axis=0, tiled=True)


def blend(axis, own_ref, other_ref, out_ref):
    sign = (1 - 2 * lax.axis_index(axis)).astype(F32)
    out_ref[...] = (own_ref[...].astype(F32) * sign + other_ref[...].astype(F32)).astype(BF16)


def pair_mixed(weight, axis):
    other = lax.ppermute(weight, axis, [(0, 1), (1, 0)])
    return call(lambda *refs: blend(axis, *refs), jax.ShapeDtypeStruct(weight.shape, BF16))(weight, other)


def shards(residual, norm_gain, gate_codes, gate_scales, up_codes, up_scales, down_codes, down_scales, hidden_signs):
    shape = jax.ShapeDtypeStruct
    columns = residual.shape[1]
    inputs = (residual, norm_gain, gate_codes, gate_scales, up_codes, up_scales, hidden_signs)
    part, own_rows = pl.pallas_call(
        project_in,
        out_shape=[shape((ROWS, WIDE), BF16), shape((OWN_ROWS, columns), BF16)],
        in_specs=[pl.BlockSpec(memory_space=pltpu.HBM)] * len(inputs),
        scratch_shapes=[pltpu.VMEM(a.shape, a.dtype) for a in inputs] + [pltpu.SemaphoreType.DMA((13,))],
        compiler_params=pltpu.CompilerParams(vmem_limit_bytes=48 << 20),
    )(*(pltpu.with_memory_space_constraint(a, pltpu.HBM) for a in inputs))
    near = exchange(part.reshape(N_NEAR, NEAR_ROWS, WIDE), NEAR)
    weight = call(rotate_down, shape((LOCAL, columns), BF16))(down_codes, down_scales)
    weight = pair_mixed(pair_mixed(weight, "c"), "zl")
    scratch = [pltpu.VMEM((NEAR_ROWS, WIDE), F32), pltpu.VMEM((NEAR_ROWS, PIECE), F32)]
    pieces = call(sum_near, shape((N_YH * N_ZH, 8, PIECE), BF16), scratch)(near)
    far = exchange(pieces, FAR)
    mixed = call(activate, shape((N_YH * N_ZH, 8, SLICE), BF16), [pltpu.VMEM((8, PIECE), F32)])(far)
    back = exchange(mixed, FAR)
    copies = call(spread_near, shape((N_NEAR, NEAR_ROWS, LOCAL), BF16), [pltpu.VMEM((NEAR_ROWS, LOCAL), F32)])(back)
    rotated = exchange(copies, NEAR).reshape(ROWS, LOCAL)
    partial = call(project_out, shape((ROWS, columns), BF16))(rotated, weight)
    sums = exchange(partial.reshape(N_T, OWN_ROWS, columns), TENSOR)
    out = call(finish, shape((N_T, OWN_ROWS, columns), BF16))(sums, own_rows)
    return exchange(out, TENSOR).reshape(ROWS, columns)


def solution(mesh):
    torus = Mesh(mesh.devices.reshape(4, N_YH, 2, N_ZH, 2, 2), ("x", "yh", "yl", "zh", "zl", "c"))
    pipe = ("x", "yh", "yl")
    placed = (
        P(None, pipe),
        P(pipe),
        P(pipe, TENSOR),
        P(pipe, TENSOR),
        P(pipe, TENSOR),
        P(pipe, TENSOR),
        P(TENSOR, pipe),
        P(TENSOR, pipe),
        P(TENSOR),
    )
    return jax.shard_map(shards, mesh=torus, in_specs=placed, out_specs=P(None, pipe), check_vma=False)
```

time: 134 us -> 129 us (0.963)
  starting transfers between devices: 8.11 us -> 27.9 us
  blocking collectives: 89.8 us -> 70.5 us
  local copies, waits for them, and re-layouts: 7.28 us -> 0.66 us
    all_to_all x4, blocking collectives: 89.8 us -> 70.5 us  [exchange(): return lax.all_to_all(blocks, axes, split_axis=0, concat_axis=0, tiled=True)]
    ppermute x0 -> x2, waiting for transfers between devices: none -> 15.2 us  [pair_mixed(): other = lax.ppermute(weight, axis, [(0, 1), (1, 0)])]
    all_to_all x2, waiting for transfers between devices: 21.9 us -> 6.89 us  [exchange(): return lax.all_to_all(blocks, axes, split_axis=0, concat_axis=0, tiled=True)]
    all_to_all x2, starting transfers between devices: 8.11 us -> 20.5 us  [exchange(): return lax.all_to_all(blocks, axes, split_axis=0, concat_axis=0, tiled=True)]
    ppermute x0 -> x2, starting transfers between devices: none -> 7.45 us  [pair_mixed(): other = lax.ppermute(weight, axis, [(0, 1), (1, 0)])]
    unnamed x17 -> x5, local copies, waits for them, and re-layouts: 5.92 us -> 0.66 us
    broadcast_in_dim x2 -> x0, local copies, waits for them, and re-layouts: 1.36 us -> none  [the longest x1 0.7 us: shards(): hidden_signs[None, :]]
    pallas_call x6 -> x8, Pallas kernels: 5.65 us -> 6.88 us  [the longest x1 3.6 us: shards(): pl.pallas_call(project_in, out_shape=[shape((ROWS, WIDE), BF16), shape((O...]
  transfers between devices with their start and end apart: 2 -> 4, of which waited for: 2 -> 2; matrix products, arithmetic and copies ran while one was open for 0% -> 0% of each run, Pallas kernels for 0% -> 2%
where the time goes in v2:
time: 129 us
  blocking collectives  70.5 us (55%)
  starting transfers between devices  27.9 us (22%)
  waiting for transfers between devices  22.1 us (17%)
  Pallas kernels  7.41 us (6%)
    all_to_all x4, blocking collectives, exchange(): return lax.all_to_all(blocks, axes, split_axis=0, concat_axis=0, tiled=True)  70.5 us
    all_to_all x2, starting transfers between devices, exchange(): return lax.all_to_all(blocks, axes, split_axis=0, concat_axis=0, tiled=True)  20.5 us
    ppermute x2, waiting for transfers between devices, pair_mixed(): other = lax.ppermute(weight, axis, [(0, 1), (1, 0)])  15.2 us
    ppermute x2, starting transfers between devices, pair_mixed(): other = lax.ppermute(weight, axis, [(0, 1), (1, 0)])  7.45 us
    all_to_all x2, waiting for transfers between devices, exchange(): return lax.all_to_all(blocks, axes, split_axis=0, concat_axis=0, tiled=True)  6.89 us
    pallas_call x1, Pallas kernels, shards(): pl.pallas_call(project_in, out_shape=[shape((ROWS, WIDE), BF16), shape((O...  3.6 us
  transfers between devices with their start and end apart: 4, of which 2 were waited for; matrix products, arithmetic and copies ran while one was open for 0% of the time, Pallas kernels for 2%

profile of v2, /device:TPU:1, one launch (start us, length us, event | category | flops | bytes accessed | tf_op | source)
XLA Modules:
  0.0 128.8 jit_solution(7862712126709571904)
XLA Ops:
  0.0 3.6 %shard_map.91 = (bf16[256,3456]{1,0:T(8,128)(2,1)S(1)}, bf16[16,256]{1,0:T(8,128)(2,1)S(1)}) custom-call(bf16[256,256]{1,0:T(8,128)(2,1)} %x_hbm.1, bf16[256]{0:T(256)(128)(2,1)} %gain_hbm.1, s32[128,1664]{1,0:T(8,128)} %gate_hbm.1, bf16[2,1664]{1,0:T(2,128)(2,1)} %gate_scales_hbm.1, s32[128,1664]{1,0:T(8,128)} %up_hbm.1, bf16[2,1664]{1,0:T(2,128)(2,1)} %up_scales_hbm.1, ...), custom_call_target="tpu_custom_call" | custom-call | tf_op jit(solution)/shard_map/pallas_call | solution.py:213
  3.6 25.7 %all_to_all.30.parts = bf16[8,32,3456]{2,1,0:T(8,128)(2,1)S(1)} all-to-all(bf16[8,32,3456]{2,1,0:T(8,128)(2,1)S(1)} %bitcast.5), channel_id=1, replica_groups=mesh['x'=4,'yh'=4,'yl'=2,'zh'=4,'zl'=2,'c'=2] {'x','yl'}, dimensions={0} | all-to-all | bytes 3538944 | tf_op jit(solution)/shard_map/all_to_all | solution.py:196
  29.3 0.0 copy-start
  29.3 0.0 copy-start.1
  29.3 1.0 shard_map.92
  30.3 16.9 %all-to-all-start.1 = ((bf16[16,8,896]{2,1,0:T(8,128)(2,1)}), bf16[16,8,896]{2,1,0:T(8,128)(2,1)S(1)}, u32[]{:S(2)}, u32[]{:S(2)}) async-start(bf16[16,8,896]{2,1,0:T(8,128)(2,1)} %shard_map.92), calls=%async_computation.1 | async-start | bytes 458752 | tf_op jit(solution)/shard_map/all_to_all | solution.py:196
  47.2 0.0 copy-done
  47.3 0.0 copy-done.1
  47.3 0.5 shard_map.95.refs_0_
  47.8 4.3 %collective-permute-start = (bf16[1664,256]{1,0:T(8,128)(2,1)S(1)}, bf16[1664,256]{1,0:T(8,128)(2,1)S(1)}, u32[]{:S(2)}, u32[]{:S(2)}) collective-permute-start(bf16[1664,256]{1,0:T(8,128)(2,1)S(1)} %shard_map.95.refs_0_), channel_id=1, source_target_pairs={{0,1},{1,0},{2,3},{3,2},{4,5},{5,4},{6,7},{7,6},{8,9},{9,8},{10,11... | collective-permute-start | bytes 2555912 | tf_op jit(solution)/shard_map/ppermute | solution.py:205
  52.1 6.9 %all-to-all-done.1.parts = bf16[16,8,896]{2,1,0:T(8,128)(2,1)S(1)} async-done(((bf16[16,8,896]{2,1,0:T(8,128)(2,1)}), bf16[16,8,896]{2,1,0:T(8,128)(2,1)S(1)}, u32[]{:S(2)}, u32[]{:S(2)}) %all-to-all-start.1) | async-done | bytes 229408 | tf_op jit(solution)/shard_map/all_to_all | solution.py:196
  59.0 0.2 shard_map.93
  59.2 16.1 %all_to_all.31.parts = bf16[16,8,416]{2,1,0:T(8,128)(2,1)S(1)} all-to-all(bf16[16,8,416]{2,1,0:T(8,128)(2,1)S(1)} %shard_map.93), channel_id=1, replica_groups=mesh['x'=4,'yh'=4,'yl'=2,'zh'=4,'zl'=2,'c'=2] {'yh','zh'}, dimensions={0} | all-to-all | bytes 212992 | tf_op jit(solution)/shard_map/all_to_all | solution.py:196
  75.4 1.1 shard_map.94
  76.5 3.5 %all-to-all-start.3 = ((bf16[8,32,1664]{2,1,0:T(8,128)(2,1)}), bf16[8,32,1664]{2,1,0:T(8,128)(2,1)S(1)}, u32[]{:S(2)}, u32[]{:S(2)}) async-start(bf16[8,32,1664]{2,1,0:T(8,128)(2,1)} %shard_map.94), calls=%async_computation.3 | async-start | bytes 1703936 | tf_op jit(solution)/shard_map/all_to_all | solution.py:196
  80.0 0.0 collective-permute-done.refs_1_
  80.0 0.3 shard_map.96.refs_0_
  80.3 3.1 %collective-permute-start.1 = (bf16[1664,256]{1,0:T(8,128)(2,1)S(1)}, bf16[1664,256]{1,0:T(8,128)(2,1)S(1)}, u32[]{:S(2)}, u32[]{:S(2)}) collective-permute-start(bf16[1664,256]{1,0:T(8,128)(2,1)S(1)} %shard_map.96.refs_0_), channel_id=1, source_target_pairs={{0,2},{2,0},{1,3},{3,1},{4,6},{6,4},{5,7},{7,5},{8,10},{10,8},{9,1... | collective-permute-start | bytes 2555912 | tf_op jit(solution)/shard_map/ppermute | solution.py:205
  83.4 15.2 %collective-permute-done.1.refs_1_ = bf16[1664,256]{1,0:T(8,128)(2,1)S(1)} collective-permute-done((bf16[1664,256]{1,0:T(8,128)(2,1)S(1)}, bf16[1664,256]{1,0:T(8,128)(2,1)S(1)}, u32[]{:S(2)}, u32[]{:S(2)}) %collective-permute-start.1) | collective-permute-done | bytes 852000 | tf_op jit(solution)/shard_map/ppermute | solution.py:205
  98.7 0.3 shard_map.97.weight
  98.9 0.0 all-to-all-done.3
  98.9 0.4 shard_map.98
  99.4 17.2 %all_to_all.32.parts = bf16[16,16,256]{2,1,0:T(8,128)(2,1)S(1)} all-to-all(bf16[16,16,256]{2,1,0:T(8,128)(2,1)S(1)} %bitcast.6), channel_id=1, replica_groups=mesh['x'=4,'yh'=4,'yl'=2,'zh'=4,'zl'=2,'c'=2] {'zh','zl','c'}, dimensions={0} | all-to-all | bytes 262144 | tf_op jit(solution)/shard_map/all_to_all | solution.py:196
  116.5 11.6 %all_to_all.33 = bf16[16,16,256]{2,1,0:T(8,128)(2,1)S(1)} all-to-all(bf16[16,16,256]{2,1,0:T(8,128)(2,1)S(1)} %shard_map.99), channel_id=1, replica_groups=mesh['x'=4,'yh'=4,'yl'=2,'zh'=4,'zl'=2,'c'=2] {'zh','zl','c'}, dimensions={0} | all-to-all | bytes 262144 | tf_op jit(solution)/shard_map/all_to_all | solution.py:196
  128.1 0.7 copy.11
  (1 shorter events, 0.0 us)
Async XLA Ops:
  29.3 17.9 %copy-start = (s32[832,256]{1,0:T(8,128)S(1)}, s32[832,256]{1,0:T(8,128)}, u32[]{:S(2)}) copy-start(s32[832,256]{1,0:T(8,128)} %codes.1) | copy-start | bytes 2555908
  29.3 17.9 %copy-start.1 = (bf16[13,256]{1,0:T(8,128)(2,1)S(1)}, bf16[13,256]{1,0:T(8,128)(2,1)}, u32[]{:S(2)}) copy-start(bf16[13,256]{1,0:T(8,128)(2,1)} %scales.1) | copy-start | bytes 19972
  30.3 28.7 %all-to-all-start.1 = ((bf16[16,8,896]{2,1,0:T(8,128)(2,1)}), bf16[16,8,896]{2,1,0:T(8,128)(2,1)S(1)}, u32[]{:S(2)}, u32[]{:S(2)}) async-start(bf16[16,8,896]{2,1,0:T(8,128)(2,1)} %shard_map.92), calls=%async_computation.1 | async-start | bytes 458752 | tf_op jit(solution)/shard_map/all_to_all | solution.py:196
  47.8 32.2 %collective-permute-start = (bf16[1664,256]{1,0:T(8,128)(2,1)S(1)}, bf16[1664,256]{1,0:T(8,128)(2,1)S(1)}, u32[]{:S(2)}, u32[]{:S(2)}) collective-permute-start(bf16[1664,256]{1,0:T(8,128)(2,1)S(1)} %shard_map.95.refs_0_), channel_id=1, source_target_pairs={{0,1},{1,0},{2,3},{3,2},{4,5},{5,4},{6,7},{7,6},{8,9},{9,8},{10,11... | collective-permute-start | bytes 2555912 | tf_op jit(solution)/shard_map/ppermute | solution.py:205
  76.5 22.5 %all-to-all-start.3 = ((bf16[8,32,1664]{2,1,0:T(8,128)(2,1)}), bf16[8,32,1664]{2,1,0:T(8,128)(2,1)S(1)}, u32[]{:S(2)}, u32[]{:S(2)}) async-start(bf16[8,32,1664]{2,1,0:T(8,128)(2,1)} %shard_map.94), calls=%async_computation.3 | async-start | bytes 1703936 | tf_op jit(solution)/shard_map/all_to_all | solution.py:196
  80.3 18.4 %collective-permute-start.1 = (bf16[1664,256]{1,0:T(8,128)(2,1)S(1)}, bf16[1664,256]{1,0:T(8,128)(2,1)S(1)}, u32[]{:S(2)}, u32[]{:S(2)}) collective-permute-start(bf16[1664,256]{1,0:T(8,128)(2,1)S(1)} %shard_map.96.refs_0_), channel_id=1, source_target_pairs={{0,2},{2,0},{1,3},{3,1},{4,6},{6,4},{5,7},{7,5},{8,10},{10,8},{9,1... | collective-permute-start | bytes 2555912 | tf_op jit(solution)/shard_map/ppermute | solution.py:205

commit v3 on v2

--- a/solution.py
+++ b/solution.py
@@ -50,8 +50,8 @@
     return jnp.where(lane == 0, coarse, jnp.where(lane == 1, value - coarse, 0.0))
 
 
-def project_in(x_hbm, gain_hbm, gate_hbm, gate_scales_hbm, up_hbm, up_scales_hbm, signs_hbm, out_ref, own_ref, *scratch):
-    x_ref, gain_ref, gate_codes, gate_scales, up_codes, up_scales, signs, sems = scratch
+def project_in(x_hbm, gain_hbm, gate_hbm, gate_scales_hbm, up_hbm, up_scales_hbm, signs_hbm, out_hbm, own_ref, *scratch):
+    out_ref, out_sems, x_ref, gain_ref, gate_codes, gate_scales, up_codes, up_scales, signs, sems = scratch
     small = [
         pltpu.make_async_copy(source, target, sems.at[i])
         for i, (source, target) in enumerate(
@@ -86,6 +86,14 @@
     ordered = jnp.dot(scaled, order, preferred_element_type=F32).astype(BF16)
     squares = jnp.sum(wide * wide, axis=1, keepdims=True)
     out_ref[:, pl.ds(2 * LOCAL, 128)] = two_parts(squares, 128).astype(BF16)
+    leaving = []
+
+    def leave(first, width):
+        lanes = pl.ds(first, width)
+        leaving.append(pltpu.make_async_copy(out_ref.at[:, lanes], out_hbm.at[:, lanes], out_sems.at[len(leaving)]))
+        leaving[-1].start()
+
+    leave(2 * LOCAL, 128)
     own_ref[...] = x_ref[pl.ds(pl.multiple_of(my_t * OWN_ROWS, OWN_ROWS), OWN_ROWS), :]
 
     for which, (codes, scales, base) in enumerate(((gate_codes, gate_scales, 0), (up_codes, up_scales, LOCAL))):
@@ -103,6 +111,11 @@
             weight = jnp.concatenate([low, high], axis=0)
             part = jnp.dot(ordered, weight, preferred_element_type=F32)
             out_ref[:, pl.ds(base + block * FACTOR, FACTOR)] = part.astype(BF16)
+            if block + 1 in starts:
+                first = starts[starts.index(block + 1) - 1]
+                leave(base + first * FACTOR, (block + 1 - first) * FACTOR)
+    for copy in leaving:
+        copy.wait()
 
 
 def rotate_down(codes, scales, out_ref):
@@ -140,7 +153,11 @@
             out_ref[yh * N_ZH + piece] = value[8 * yh : 8 * yh + 8, :]
 
 
-def activate(parts, out_ref, joined):
+def source_of(shift):
+    return lax.rem(lax.axis_index("zh") + N_ZH - shift, N_ZH)
+
+
+def activate(parts, out_ref, joined, mixed, ordered):
     values = []
     inverse = None
     for z in range(N_ZH):
@@ -163,24 +180,28 @@
         ]
         step *= 2
     for z in range(N_ZH):
-        mixed = values[z].astype(BF16)
-        for yh in range(N_YH):
-            out_ref[yh * N_ZH + z] = mixed
-
-
-def spread_near(parts, out_ref, joined):
-    for piece in range(N_ZH):
-        for yh in range(N_YH):
-            joined[8 * yh : 8 * yh + 8, piece * SLICE : (piece + 1) * SLICE] = parts[yh * N_ZH + piece].astype(F32)
+        mixed[z] = values[z]
+    for j in range(N_ZH):
+        ordered[:, j * SLICE : (j + 1) * SLICE] = mixed[source_of(j)]
     for block in range(BLOCKS):
         lanes = pl.ds(block * 128, 128)
-        value = joined[:, lanes].astype(BF16)
+        value = ordered[:, lanes].astype(BF16)
+        for target in range(out_ref.shape[0]):
+            out_ref[target, :, lanes] = value
+
+
+def spread_near(parts, out_ref):
+    for yh in range(N_YH):
+        value = parts[yh]
         for target in range(N_NEAR):
-            out_ref[target, :, lanes] = value
-
-
-def project_out(act, weight, out_ref):
-    out_ref[...] = jnp.dot(act[...], weight[...], preferred_element_type=F32).astype(BF16)
+            out_ref[target, 8 * yh : 8 * yh + 8, :] = value
+
+
+def project_out(act, *refs):
+    weights, (out_ref, joined) = refs[:N_ZH], refs[N_ZH:]
+    for j in range(N_ZH):
+        joined[pl.ds(j * SLICE, SLICE), :] = weights[j][...]
+    out_ref[...] = jnp.dot(act[...], joined[...], preferred_element_type=F32).astype(BF16)
 
 
 def finish(parts, residual, out_ref):
@@ -196,14 +217,24 @@
     return lax.all_to_all(blocks, axes, split_axis=0, concat_axis=0, tiled=True)
 
 
-def blend(axis, own_ref, other_ref, out_ref):
+def blended(axis, own, other):
     sign = (1 - 2 * lax.axis_index(axis)).astype(F32)
-    out_ref[...] = (own_ref[...].astype(F32) * sign + other_ref[...].astype(F32)).astype(BF16)
-
-
-def pair_mixed(weight, axis):
-    other = lax.ppermute(weight, axis, [(0, 1), (1, 0)])
-    return call(lambda *refs: blend(axis, *refs), jax.ShapeDtypeStruct(weight.shape, BF16))(weight, other)
+    return (own.astype(F32) * sign + other.astype(F32)).astype(BF16)
+
+
+def swapped(weight, axis):
+    return lax.ppermute(weight, axis, [(0, 1), (1, 0)])
+
+
+def blend_core(own_ref, other_ref, out_ref):
+    out_ref[...] = blended("c", own_ref[...], other_ref[...])
+
+
+def blend_chip(own_ref, other_ref, *out_refs):
+    for j in range(N_ZH):
+        group = lax.rem(lax.axis_index("zh") + j, N_ZH)
+        rows = pl.ds(pl.multiple_of(group * SLICE, SLICE), SLICE)
+        out_refs[j][...] = blended("zl", own_ref[rows, :], other_ref[rows, :])
 
 
 def shards(residual, norm_gain, gate_codes, gate_scales, up_codes, up_scales, down_codes, down_scales, hidden_signs):
@@ -214,20 +245,29 @@
         project_in,
         out_shape=[shape((ROWS, WIDE), BF16), shape((OWN_ROWS, columns), BF16)],
         in_specs=[pl.BlockSpec(memory_space=pltpu.HBM)] * len(inputs),
-        scratch_shapes=[pltpu.VMEM(a.shape, a.dtype) for a in inputs] + [pltpu.SemaphoreType.DMA((13,))],
+        out_specs=[pl.BlockSpec(memory_space=pltpu.HBM), pl.BlockSpec(memory_space=pltpu.VMEM)],
+        scratch_shapes=[pltpu.VMEM((ROWS, WIDE), BF16), pltpu.SemaphoreType.DMA((9,))]
+        + [pltpu.VMEM(a.shape, a.dtype) for a in inputs] + [pltpu.SemaphoreType.DMA((13,))],
         compiler_params=pltpu.CompilerParams(vmem_limit_bytes=48 << 20),
     )(*(pltpu.with_memory_space_constraint(a, pltpu.HBM) for a in inputs))
     near = exchange(part.reshape(N_NEAR, NEAR_ROWS, WIDE), NEAR)
     weight = call(rotate_down, shape((LOCAL, columns), BF16))(down_codes, down_scales)
-    weight = pair_mixed(pair_mixed(weight, "c"), "zl")
+    other = swapped(weight, "c")
+    weight = call(blend_core, shape(weight.shape, BF16))(weight, other)
+    other = swapped(weight, "zl")
+    groups = call(blend_chip, [shape((SLICE, columns), BF16)] * N_ZH)(weight, other)
+    weights = [groups[0]]
+    for j in range(1, N_ZH):
+        weights.append(lax.ppermute(groups[j], "zh", [(i, (i + j) % N_ZH) for i in range(N_ZH)]))
     scratch = [pltpu.VMEM((NEAR_ROWS, WIDE), F32), pltpu.VMEM((NEAR_ROWS, PIECE), F32)]
     pieces = call(sum_near, shape((N_YH * N_ZH, 8, PIECE), BF16), scratch)(near)
     far = exchange(pieces, FAR)
-    mixed = call(activate, shape((N_YH * N_ZH, 8, SLICE), BF16), [pltpu.VMEM((8, PIECE), F32)])(far)
-    back = exchange(mixed, FAR)
-    copies = call(spread_near, shape((N_NEAR, NEAR_ROWS, LOCAL), BF16), [pltpu.VMEM((NEAR_ROWS, LOCAL), F32)])(back)
+    scratch = [pltpu.VMEM((8, PIECE), F32), pltpu.VMEM((N_ZH, 8, SLICE), F32), pltpu.VMEM((8, LOCAL), F32)]
+    mixed = call(activate, shape((N_YH, 8, LOCAL), BF16), scratch)(far)
+    back = exchange(mixed, "yh")
+    copies = call(spread_near, shape((N_NEAR, NEAR_ROWS, LOCAL), BF16))(back)
     rotated = exchange(copies, NEAR).reshape(ROWS, LOCAL)
-    partial = call(project_out, shape((ROWS, columns), BF16))(rotated, weight)
+    partial = call(project_out, shape((ROWS, columns), BF16), [pltpu.VMEM((LOCAL, columns), BF16)])(rotated, *weights)
     sums = exchange(partial.reshape(N_T, OWN_ROWS, columns), TENSOR)
     out = call(finish, shape((N_T, OWN_ROWS, columns), BF16))(sums, own_rows)
     return exchange(out, TENSOR).reshape(ROWS, columns)

time: 129 us -> 149 us (1.16)
  waiting for transfers between devices: 22.1 us -> 40.4 us
  starting transfers between devices: 27.9 us -> 38.4 us
  blocking collectives: 70.5 us -> 61.5 us
    ppermute x2 -> x5, waiting for transfers between devices: 15.2 us -> 33.5 us  [the longest x3 18.3 us: shards(): lax.ppermute(groups[j], 'zh', [(i, (i + j) % N_ZH) for i in range(N_ZH)])]
    ppermute x2 -> x5, starting transfers between devices: 7.45 us -> 17.9 us  [the longest x3 10.7 us: shards(): lax.ppermute(groups[j], 'zh', [(i, (i + j) % N_ZH) for i in range(N_ZH)])]
    all_to_all x4, blocking collectives: 70.5 us -> 61.5 us  [exchange(): return lax.all_to_all(blocks, axes, split_axis=0, concat_axis=0, tiled=True)]
  transfers between devices with their start and end apart: 4 -> 7, of which waited for: 2 -> 4; matrix products, arithmetic and copies ran while one was open for 0% -> 0% of each run, Pallas kernels for 2% -> 2%
where the time goes in v3:
time: 149 us
  blocking collectives  61.5 us (41%)
  waiting for transfers between devices  40.4 us (27%)
  starting transfers between devices  38.4 us (26%)
  Pallas kernels  7.66 us (5%)
    all_to_all x4, blocking collectives, exchange(): return lax.all_to_all(blocks, axes, split_axis=0, concat_axis=0, tiled=True)  61.5 us
    all_to_all x2, starting transfers between devices, exchange(): return lax.all_to_all(blocks, axes, split_axis=0, concat_axis=0, tiled=True)  20.5 us
    ppermute x3, waiting for transfers between devices, shards(): lax.ppermute(groups[j], 'zh', [(i, (i + j) % N_ZH) for i in range(N_ZH)])  18.3 us
    ppermute x2, waiting for transfers between devices, swapped(): return lax.ppermute(weight, axis, [(0, 1), (1, 0)])  15.2 us
    ppermute x3, starting transfers between devices, shards(): lax.ppermute(groups[j], 'zh', [(i, (i + j) % N_ZH) for i in range(N_ZH)])  10.7 us
    ppermute x2, starting transfers between devices, swapped(): return lax.ppermute(weight, axis, [(0, 1), (1, 0)])  7.19 us
    all_to_all x2, waiting for transfers between devices, exchange(): return lax.all_to_all(blocks, axes, split_axis=0, concat_axis=0, tiled=True)  6.9 us
    pallas_call x1, Pallas kernels, shards(): pl.pallas_call(project_in, out_shape=[shape((ROWS, WIDE), BF16), shape((O...  3.85 us
  transfers between devices with their start and end apart: 7, of which 4 were waited for; matrix products, arithmetic and copies ran while one was open for 0% of the time, Pallas kernels for 2%

profile of v3, /device:TPU:1, one launch (start us, length us, event | category | flops | bytes accessed | tf_op | source)
XLA Modules:
  0.0 148.7 jit_solution(16610996363290319401)
XLA Ops:
  0.0 3.9 %shard_map.91 = (bf16[256,3456]{1,0:T(8,128)(2,1)S(1)}, bf16[16,256]{1,0:T(8,128)(2,1)S(1)}) custom-call(bf16[256,256]{1,0:T(8,128)(2,1)} %x_hbm.1, bf16[256]{0:T(256)(128)(2,1)} %gain_hbm.1, s32[128,1664]{1,0:T(8,128)} %gate_hbm.1, bf16[2,1664]{1,0:T(2,128)(2,1)} %gate_scales_hbm.1, s32[128,1664]{1,0:T(8,128)} %up_hbm.1, bf16[2,1664]{1,0:T(2,128)(2,1)} %up_scales_hbm.1, ...), custom_call_target="tpu_custom_call" | custom-call | tf_op jit(solution)/shard_map/pallas_call | solution.py:244
  3.9 25.7 %all_to_all.30.parts = bf16[8,32,3456]{2,1,0:T(8,128)(2,1)S(1)} all-to-all(bf16[8,32,3456]{2,1,0:T(8,128)(2,1)S(1)} %bitcast.5), channel_id=1, replica_groups=mesh['x'=4,'yh'=4,'yl'=2,'zh'=4,'zl'=2,'c'=2] {'x','yl'}, dimensions={0} | all-to-all | bytes 3538944 | tf_op jit(solution)/shard_map/all_to_all | solution.py:217
  29.6 0.0 copy-start
  29.6 0.0 copy-start.1
  29.6 1.0 shard_map.92
  30.6 16.9 %all-to-all-start.1 = ((bf16[16,8,896]{2,1,0:T(8,128)(2,1)}), bf16[16,8,896]{2,1,0:T(8,128)(2,1)S(1)}, u32[]{:S(2)}, u32[]{:S(2)}) async-start(bf16[16,8,896]{2,1,0:T(8,128)(2,1)} %shard_map.92), calls=%async_computation.1 | async-start | bytes 458752 | tf_op jit(solution)/shard_map/all_to_all | solution.py:217
  47.5 0.0 copy-done
  47.5 0.0 copy-done.1
  47.5 0.5 shard_map.95.own_ref
  48.1 4.3 %collective-permute-start = (bf16[1664,256]{1,0:T(8,128)(2,1)S(1)}, bf16[1664,256]{1,0:T(8,128)(2,1)S(1)}, u32[]{:S(2)}, u32[]{:S(2)}) collective-permute-start(bf16[1664,256]{1,0:T(8,128)(2,1)S(1)} %shard_map.95.own_ref), channel_id=1, source_target_pairs={{0,1},{1,0},{2,3},{3,2},{4,5},{5,4},{6,7},{7,6},{8,9},{9,8},{10,11... | collective-permute-start | bytes 2555912 | tf_op jit(solution)/shard_map/ppermute | solution.py:226
  52.4 6.9 %all-to-all-done.1.parts = bf16[16,8,896]{2,1,0:T(8,128)(2,1)S(1)} async-done(((bf16[16,8,896]{2,1,0:T(8,128)(2,1)}), bf16[16,8,896]{2,1,0:T(8,128)(2,1)S(1)}, u32[]{:S(2)}, u32[]{:S(2)}) %all-to-all-start.1) | async-done | bytes 229408 | tf_op jit(solution)/shard_map/all_to_all | solution.py:217
  59.3 0.3 shard_map.93
  59.6 10.5 %all_to_all.31.parts = bf16[4,8,1664]{2,1,0:T(8,128)(2,1)S(1)} all-to-all(bf16[4,8,1664]{2,1,0:T(8,128)(2,1)S(1)} %shard_map.93), channel_id=1, replica_groups=mesh['x'=4,'yh'=4,'yl'=2,'zh'=4,'zl'=2,'c'=2] {'yh'}, dimensions={0} | all-to-all | bytes 212992 | tf_op jit(solution)/shard_map/all_to_all | solution.py:217
  70.1 1.0 shard_map.94
  71.1 3.5 %all-to-all-start.3 = ((bf16[8,32,1664]{2,1,0:T(8,128)(2,1)}), bf16[8,32,1664]{2,1,0:T(8,128)(2,1)S(1)}, u32[]{:S(2)}, u32[]{:S(2)}) async-start(bf16[8,32,1664]{2,1,0:T(8,128)(2,1)} %shard_map.94), calls=%async_computation.3 | async-start | bytes 1703936 | tf_op jit(solution)/shard_map/all_to_all | solution.py:217
  74.6 0.0 collective-permute-done.other_ref
  74.7 0.3 shard_map.96.own_ref
  74.9 2.9 %collective-permute-start.1 = (bf16[1664,256]{1,0:T(8,128)(2,1)S(1)}, bf16[1664,256]{1,0:T(8,128)(2,1)S(1)}, u32[]{:S(2)}, u32[]{:S(2)}) collective-permute-start(bf16[1664,256]{1,0:T(8,128)(2,1)S(1)} %shard_map.96.own_ref), channel_id=1, source_target_pairs={{0,2},{2,0},{1,3},{3,1},{4,6},{6,4},{5,7},{7,5},{8,10},{10,8},{9,1... | collective-permute-start | bytes 2555912 | tf_op jit(solution)/shard_map/ppermute | solution.py:226
  77.8 15.2 %collective-permute-done.1.other_ref = bf16[1664,256]{1,0:T(8,128)(2,1)S(1)} collective-permute-done((bf16[1664,256]{1,0:T(8,128)(2,1)S(1)}, bf16[1664,256]{1,0:T(8,128)(2,1)S(1)}, u32[]{:S(2)}, u32[]{:S(2)}) %collective-permute-start.1) | collective-permute-done | bytes 852000 | tf_op jit(solution)/shard_map/ppermute | solution.py:226
  93.0 0.3 shard_map.97
  93.2 3.2 %collective-permute-start.2 = (bf16[416,256]{1,0:T(8,128)(2,1)S(1)}, bf16[416,256]{1,0:T(8,128)(2,1)S(1)}, u32[]{:S(2)}, u32[]{:S(2)}) collective-permute-start(bf16[416,256]{1,0:T(8,128)(2,1)S(1)} %get-tuple-element.13), channel_id=1, source_target_pairs={{0,4},{4,8},{8,12},{12,0},{1,5},{5,9},{9,13},{13,1},{2,6},{6,10},{... | collective-permute-start | bytes 638984 | tf_op jit(solution)/shard_map/ppermute | solution.py:261
  96.5 2.4 %collective-permute-start.3 = (bf16[416,256]{1,0:T(8,128)(2,1)S(1)}, bf16[416,256]{1,0:T(8,128)(2,1)S(1)}, u32[]{:S(2)}, u32[]{:S(2)}) collective-permute-start(bf16[416,256]{1,0:T(8,128)(2,1)S(1)} %get-tuple-element.14), channel_id=1, source_target_pairs={{0,8},{4,12},{8,0},{12,4},{1,9},{5,13},{9,1},{13,5},{2,10},{6,14},... | collective-permute-start | bytes 638984 | tf_op jit(solution)/shard_map/ppermute | solution.py:261
  98.9 5.1 %collective-permute-start.4 = (bf16[416,256]{1,0:T(8,128)(2,1)S(1)}, bf16[416,256]{1,0:T(8,128)(2,1)S(1)}, u32[]{:S(2)}, u32[]{:S(2)}) collective-permute-start(bf16[416,256]{1,0:T(8,128)(2,1)S(1)} %get-tuple-element.15), channel_id=1, source_target_pairs={{0,12},{4,0},{8,4},{12,8},{1,13},{5,1},{9,5},{13,9},{2,14},{6,2},{... | collective-permute-start | bytes 638984 | tf_op jit(solution)/shard_map/ppermute | solution.py:261
  104.0 0.0 collective-permute-done.2.refs_1_
  104.0 10.1 %collective-permute-done.3.refs_2_ = bf16[416,256]{1,0:T(8,128)(2,1)S(1)} collective-permute-done((bf16[416,256]{1,0:T(8,128)(2,1)S(1)}, bf16[416,256]{1,0:T(8,128)(2,1)S(1)}, u32[]{:S(2)}, u32[]{:S(2)}) %collective-permute-start.3) | collective-permute-done | bytes 213024 | tf_op jit(solution)/shard_map/ppermute | solution.py:261
  114.1 8.2 %collective-permute-done.4.refs_3_ = bf16[416,256]{1,0:T(8,128)(2,1)S(1)} collective-permute-done((bf16[416,256]{1,0:T(8,128)(2,1)S(1)}, bf16[416,256]{1,0:T(8,128)(2,1)S(1)}, u32[]{:S(2)}, u32[]{:S(2)}) %collective-permute-start.4) | collective-permute-done | bytes 213024 | tf_op jit(solution)/shard_map/ppermute | solution.py:261
  122.3 0.0 all-to-all-done.3
  122.3 0.4 shard_map.98
  122.7 13.7 %all_to_all.32.parts = bf16[16,16,256]{2,1,0:T(8,128)(2,1)S(1)} all-to-all(bf16[16,16,256]{2,1,0:T(8,128)(2,1)S(1)} %bitcast.6), channel_id=1, replica_groups=mesh['x'=4,'yh'=4,'yl'=2,'zh'=4,'zl'=2,'c'=2] {'zh','zl','c'}, dimensions={0} | all-to-all | bytes 262144 | tf_op jit(solution)/shard_map/all_to_all | solution.py:217
  136.5 11.6 %all_to_all.33 = bf16[16,16,256]{2,1,0:T(8,128)(2,1)S(1)} all-to-all(bf16[16,16,256]{2,1,0:T(8,128)(2,1)S(1)} %shard_map.99), channel_id=1, replica_groups=mesh['x'=4,'yh'=4,'yl'=2,'zh'=4,'zl'=2,'c'=2] {'zh','zl','c'}, dimensions={0} | all-to-all | bytes 262144 | tf_op jit(solution)/shard_map/all_to_all | solution.py:217
  148.0 0.7 copy.11
  (1 shorter events, 0.0 us)
Async XLA Ops:
  29.6 17.9 %copy-start = (s32[832,256]{1,0:T(8,128)S(1)}, s32[832,256]{1,0:T(8,128)}, u32[]{:S(2)}) copy-start(s32[832,256]{1,0:T(8,128)} %codes.1) | copy-start | bytes 2555908
  29.6 18.0 %copy-start.1 = (bf16[13,256]{1,0:T(8,128)(2,1)S(1)}, bf16[13,256]{1,0:T(8,128)(2,1)}, u32[]{:S(2)}) copy-start(bf16[13,256]{1,0:T(8,128)(2,1)} %scales.1) | copy-start | bytes 19972
  30.6 28.7 %all-to-all-start.1 = ((bf16[16,8,896]{2,1,0:T(8,128)(2,1)}), bf16[16,8,896]{2,1,0:T(8,128)(2,1)S(1)}, u32[]{:S(2)}, u32[]{:S(2)}) async-start(bf16[16,8,896]{2,1,0:T(8,128)(2,1)} %shard_map.92), calls=%async_computation.1 | async-start | bytes 458752 | tf_op jit(solution)/shard_map/all_to_all | solution.py:217
  48.1 26.6 %collective-permute-start = (bf16[1664,256]{1,0:T(8,128)(2,1)S(1)}, bf16[1664,256]{1,0:T(8,128)(2,1)S(1)}, u32[]{:S(2)}, u32[]{:S(2)}) collective-permute-start(bf16[1664,256]{1,0:T(8,128)(2,1)S(1)} %shard_map.95.own_ref), channel_id=1, source_target_pairs={{0,1},{1,0},{2,3},{3,2},{4,5},{5,4},{6,7},{7,6},{8,9},{9,8},{10,11... | collective-permute-start | bytes 2555912 | tf_op jit(solution)/shard_map/ppermute | solution.py:226
  71.1 51.2 %all-to-all-start.3 = ((bf16[8,32,1664]{2,1,0:T(8,128)(2,1)}), bf16[8,32,1664]{2,1,0:T(8,128)(2,1)S(1)}, u32[]{:S(2)}, u32[]{:S(2)}) async-start(bf16[8,32,1664]{2,1,0:T(8,128)(2,1)} %shard_map.94), calls=%async_computation.3 | async-start | bytes 1703936 | tf_op jit(solution)/shard_map/all_to_all | solution.py:217
  74.9 18.1 %collective-permute-start.1 = (bf16[1664,256]{1,0:T(8,128)(2,1)S(1)}, bf16[1664,256]{1,0:T(8,128)(2,1)S(1)}, u32[]{:S(2)}, u32[]{:S(2)}) collective-permute-start(bf16[1664,256]{1,0:T(8,128)(2,1)S(1)} %shard_map.96.own_ref), channel_id=1, source_target_pairs={{0,2},{2,0},{1,3},{3,1},{4,6},{6,4},{5,7},{7,5},{8,10},{10,8},{9,1... | collective-permute-start | bytes 2555912 | tf_op jit(solution)/shard_map/ppermute | solution.py:226
  93.2 10.8 %collective-permute-start.2 = (bf16[416,256]{1,0:T(8,128)(2,1)S(1)}, bf16[416,256]{1,0:T(8,128)(2,1)S(1)}, u32[]{:S(2)}, u32[]{:S(2)}) collective-permute-start(bf16[416,256]{1,0:T(8,128)(2,1)S(1)} %get-tuple-element.13), channel_id=1, source_target_pairs={{0,4},{4,8},{8,12},{12,0},{1,5},{5,9},{9,13},{13,1},{2,6},{6,10},{... | collective-permute-start | bytes 638984 | tf_op jit(solution)/shard_map/ppermute | solution.py:261
  96.5 17.6 %collective-permute-start.3 = (bf16[416,256]{1,0:T(8,128)(2,1)S(1)}, bf16[416,256]{1,0:T(8,128)(2,1)S(1)}, u32[]{:S(2)}, u32[]{:S(2)}) collective-permute-start(bf16[416,256]{1,0:T(8,128)(2,1)S(1)} %get-tuple-element.14), channel_id=1, source_target_pairs={{0,8},{4,12},{8,0},{12,4},{1,9},{5,13},{9,1},{13,5},{2,10},{6,14},... | collective-permute-start | bytes 638984 | tf_op jit(solution)/shard_map/ppermute | solution.py:261
  98.9 23.4 %collective-permute-start.4 = (bf16[416,256]{1,0:T(8,128)(2,1)S(1)}, bf16[416,256]{1,0:T(8,128)(2,1)S(1)}, u32[]{:S(2)}, u32[]{:S(2)}) collective-permute-start(bf16[416,256]{1,0:T(8,128)(2,1)S(1)} %get-tuple-element.15), channel_id=1, source_target_pairs={{0,12},{4,0},{8,4},{12,8},{1,13},{5,1},{9,5},{13,9},{2,14},{6,2},{... | collective-permute-start | bytes 638984 | tf_op jit(solution)/shard_map/ppermute | solution.py:261

commit v4 on v3

--- a/solution.py
+++ b/solution.py
@@ -61,7 +61,8 @@
     for copy in small:
         copy.start()
     copies = {}
-    starts = (0, 4, 7, 10, BLOCKS)
+    starts = (0, BLOCKS)
+    ends = (0, 7, BLOCKS)
     slot = len(small)
     for which, (source, target) in enumerate(((gate_hbm, gate_codes), (up_hbm, up_codes))):
         for first, last in zip(starts[:-1], starts[1:]):
@@ -111,8 +112,8 @@
             weight = jnp.concatenate([low, high], axis=0)
             part = jnp.dot(ordered, weight, preferred_element_type=F32)
             out_ref[:, pl.ds(base + block * FACTOR, FACTOR)] = part.astype(BF16)
-            if block + 1 in starts:
-                first = starts[starts.index(block + 1) - 1]
+            if block + 1 in ends:
+                first = ends[ends.index(block + 1) - 1]
                 leave(base + first * FACTOR, (block + 1 - first) * FACTOR)
     for copy in leaving:
         copy.wait()
@@ -197,11 +198,11 @@
             out_ref[target, 8 * yh : 8 * yh + 8, :] = value
 
 
-def project_out(act, *refs):
-    weights, (out_ref, joined) = refs[:N_ZH], refs[N_ZH:]
-    for j in range(N_ZH):
-        joined[pl.ds(j * SLICE, SLICE), :] = weights[j][...]
-    out_ref[...] = jnp.dot(act[...], joined[...], preferred_element_type=F32).astype(BF16)
+def project_out(act_ref, own_ref, other_ref, out_ref):
+    act = act_ref[...]
+    own = jnp.dot(act, own_ref[...], preferred_element_type=F32)
+    other = jnp.dot(act, other_ref[...], preferred_element_type=F32)
+    out_ref[...] = (own * side("zl") + other).astype(BF16)
 
 
 def finish(parts, residual, out_ref):
@@ -217,24 +218,26 @@
     return lax.all_to_all(blocks, axes, split_axis=0, concat_axis=0, tiled=True)
 
 
-def blended(axis, own, other):
-    sign = (1 - 2 * lax.axis_index(axis)).astype(F32)
-    return (own.astype(F32) * sign + other.astype(F32)).astype(BF16)
+def side(axis):
+    return (1 - 2 * lax.axis_index(axis)).astype(F32)
 
 
 def swapped(weight, axis):
     return lax.ppermute(weight, axis, [(0, 1), (1, 0)])
 
 
-def blend_core(own_ref, other_ref, out_ref):
-    out_ref[...] = blended("c", own_ref[...], other_ref[...])
-
-
-def blend_chip(own_ref, other_ref, *out_refs):
+def blend_core(own_ref, other_ref, *out_refs):
     for j in range(N_ZH):
         group = lax.rem(lax.axis_index("zh") + j, N_ZH)
         rows = pl.ds(pl.multiple_of(group * SLICE, SLICE), SLICE)
-        out_refs[j][...] = blended("zl", own_ref[rows, :], other_ref[rows, :])
+        both = own_ref[rows, :].astype(F32) * side("c") + other_ref[rows, :].astype(F32)
+        out_refs[j][...] = both.astype(BF16)
+
+
+def join(*refs):
+    out_ref = refs[N_ZH]
+    for j in range(N_ZH):
+        out_ref[pl.ds(j * SLICE, SLICE), :] = refs[j][...]
 
 
 def shards(residual, norm_gain, gate_codes, gate_scales, up_codes, up_scales, down_codes, down_scales, hidden_signs):
@@ -246,19 +249,19 @@
         out_shape=[shape((ROWS, WIDE), BF16), shape((OWN_ROWS, columns), BF16)],
         in_specs=[pl.BlockSpec(memory_space=pltpu.HBM)] * len(inputs),
         out_specs=[pl.BlockSpec(memory_space=pltpu.HBM), pl.BlockSpec(memory_space=pltpu.VMEM)],
-        scratch_shapes=[pltpu.VMEM((ROWS, WIDE), BF16), pltpu.SemaphoreType.DMA((9,))]
-        + [pltpu.VMEM(a.shape, a.dtype) for a in inputs] + [pltpu.SemaphoreType.DMA((13,))],
+        scratch_shapes=[pltpu.VMEM((ROWS, WIDE), BF16), pltpu.SemaphoreType.DMA((5,))]
+        + [pltpu.VMEM(a.shape, a.dtype) for a in inputs] + [pltpu.SemaphoreType.DMA((7,))],
         compiler_params=pltpu.CompilerParams(vmem_limit_bytes=48 << 20),
     )(*(pltpu.with_memory_space_constraint(a, pltpu.HBM) for a in inputs))
     near = exchange(part.reshape(N_NEAR, NEAR_ROWS, WIDE), NEAR)
     weight = call(rotate_down, shape((LOCAL, columns), BF16))(down_codes, down_scales)
     other = swapped(weight, "c")
-    weight = call(blend_core, shape(weight.shape, BF16))(weight, other)
+    groups = call(blend_core, [shape((SLICE, columns), BF16)] * N_ZH)(weight, other)
+    dealt = [groups[0]]
+    for j in range(1, N_ZH):
+        dealt.append(lax.ppermute(groups[j], "zh", [(i, (i + j) % N_ZH) for i in range(N_ZH)]))
+    weight = call(join, shape((LOCAL, columns), BF16))(*dealt)
     other = swapped(weight, "zl")
-    groups = call(blend_chip, [shape((SLICE, columns), BF16)] * N_ZH)(weight, other)
-    weights = [groups[0]]
-    for j in range(1, N_ZH):
-        weights.append(lax.ppermute(groups[j], "zh", [(i, (i + j) % N_ZH) for i in range(N_ZH)]))
     scratch = [pltpu.VMEM((NEAR_ROWS, WIDE), F32), pltpu.VMEM((NEAR_ROWS, PIECE), F32)]
     pieces = call(sum_near, shape((N_YH * N_ZH, 8, PIECE), BF16), scratch)(near)
     far = exchange(pieces, FAR)
@@ -267,7 +270,7 @@
     back = exchange(mixed, "yh")
     copies = call(spread_near, shape((N_NEAR, NEAR_ROWS, LOCAL), BF16))(back)
     rotated = exchange(copies, NEAR).reshape(ROWS, LOCAL)
-    partial = call(project_out, shape((ROWS, columns), BF16), [pltpu.VMEM((LOCAL, columns), BF16)])(rotated, *weights)
+    partial = call(project_out, shape((ROWS, columns), BF16), [])(rotated, weight, other)
     sums = exchange(partial.reshape(N_T, OWN_ROWS, columns), TENSOR)
     out = call(finish, shape((N_T, OWN_ROWS, columns), BF16))(sums, own_rows)
     return exchange(out, TENSOR).reshape(ROWS, columns)

time: 149 us -> 153 us (1.027)
  waiting for transfers between devices: 40.4 us -> 45.7 us
    ppermute x2, waiting for transfers between devices: 15.2 us -> 20 us  [swapped(): return lax.ppermute(weight, axis, [(0, 1), (1, 0)])]
  transfers between devices with their start and end apart: 7 -> 7, of which waited for: 4 -> 5; matrix products, arithmetic and copies ran while one was open for 0% -> 0% of each run, Pallas kernels for 2% -> 1%
where the time goes in v4:
time: 153 us; the launch traced here: 152 us
  blocking collectives  61.2 us (40%)
  waiting for transfers between devices  45.7 us (30%)
  starting transfers between devices  37.4 us (24%)
  Pallas kernels  7.01 us (5%)
    all_to_all x4, blocking collectives, exchange(): return lax.all_to_all(blocks, axes, split_axis=0, concat_axis=0, tiled=True)  61.2 us
    all_to_all x2, starting transfers between devices, exchange(): return lax.all_to_all(blocks, axes, split_axis=0, concat_axis=0, tiled=True)  20.5 us
    ppermute x2, waiting for transfers between devices, swapped(): return lax.ppermute(weight, axis, [(0, 1), (1, 0)])  20 us
    ppermute x3, waiting for transfers between devices, shards(): lax.ppermute(groups[j], 'zh', [(i, (i + j) % N_ZH) for i in range(N_ZH)])  18.8 us
    ppermute x3, starting transfers between devices, shards(): lax.ppermute(groups[j], 'zh', [(i, (i + j) % N_ZH) for i in range(N_ZH)])  10.7 us
    all_to_all x2, waiting for transfers between devices, exchange(): return lax.all_to_all(blocks, axes, split_axis=0, concat_axis=0, tiled=True)  6.91 us
    ppermute x2, starting transfers between devices, swapped(): return lax.ppermute(weight, axis, [(0, 1), (1, 0)])  6.21 us
    pallas_call x1, Pallas kernels, shards(): pl.pallas_call(project_in, out_shape=[shape((ROWS, WIDE), BF16), shape((O...  3.16 us
  transfers between devices with their start and end apart: 7, of which 5 were waited for; matrix products, arithmetic and copies ran while one was open for 0% of the time, Pallas kernels for 1%

profile of v4, /device:TPU:1, one launch (start us, length us, event | category | flops | bytes accessed | tf_op | source)
XLA Modules:
  0.0 152.0 jit_solution(5112510814797322674)
XLA Ops:
  0.0 3.2 %shard_map.91 = (bf16[256,3456]{1,0:T(8,128)(2,1)S(1)}, bf16[16,256]{1,0:T(8,128)(2,1)S(1)}) custom-call(bf16[256,256]{1,0:T(8,128)(2,1)} %x_hbm.1, bf16[256]{0:T(256)(128)(2,1)} %gain_hbm.1, s32[128,1664]{1,0:T(8,128)} %gate_hbm.1, bf16[2,1664]{1,0:T(2,128)(2,1)} %gate_scales_hbm.1, s32[128,1664]{1,0:T(8,128)} %up_hbm.1, bf16[2,1664]{1,0:T(2,128)(2,1)} %up_scales_hbm.1, ...), custom_call_target="tpu_custom_call" | custom-call | tf_op jit(solution)/shard_map/pallas_call | solution.py:247
  3.2 25.7 %all_to_all.30.parts = bf16[8,32,3456]{2,1,0:T(8,128)(2,1)S(1)} all-to-all(bf16[8,32,3456]{2,1,0:T(8,128)(2,1)S(1)} %bitcast.5), channel_id=1, replica_groups=mesh['x'=4,'yh'=4,'yl'=2,'zh'=4,'zl'=2,'c'=2] {'x','yl'}, dimensions={0} | all-to-all | bytes 3538944 | tf_op jit(solution)/shard_map/all_to_all | solution.py:218
  28.9 0.0 copy-start
  28.9 0.0 copy-start.1
  28.9 1.0 shard_map.92
  29.9 16.9 %all-to-all-start.1 = ((bf16[16,8,896]{2,1,0:T(8,128)(2,1)}), bf16[16,8,896]{2,1,0:T(8,128)(2,1)S(1)}, u32[]{:S(2)}, u32[]{:S(2)}) async-start(bf16[16,8,896]{2,1,0:T(8,128)(2,1)} %shard_map.92), calls=%async_computation.1 | async-start | bytes 458752 | tf_op jit(solution)/shard_map/all_to_all | solution.py:218
  46.9 0.0 copy-done
  46.9 0.0 copy-done.1
  46.9 0.5 shard_map.95.own_ref
  47.4 4.3 %collective-permute-start = (bf16[1664,256]{1,0:T(8,128)(2,1)S(1)}, bf16[1664,256]{1,0:T(8,128)(2,1)S(1)}, u32[]{:S(2)}, u32[]{:S(2)}) collective-permute-start(bf16[1664,256]{1,0:T(8,128)(2,1)S(1)} %shard_map.95.own_ref), channel_id=1, source_target_pairs={{0,1},{1,0},{2,3},{3,2},{4,5},{5,4},{6,7},{7,6},{8,9},{9,8},{10,11... | collective-permute-start | bytes 2555912 | tf_op jit(solution)/shard_map/ppermute | solution.py:226
  51.7 6.9 %all-to-all-done.1.parts = bf16[16,8,896]{2,1,0:T(8,128)(2,1)S(1)} async-done(((bf16[16,8,896]{2,1,0:T(8,128)(2,1)}), bf16[16,8,896]{2,1,0:T(8,128)(2,1)S(1)}, u32[]{:S(2)}, u32[]{:S(2)}) %all-to-all-start.1) | async-done | bytes 229408 | tf_op jit(solution)/shard_map/all_to_all | solution.py:218
  58.6 0.3 shard_map.93
  58.9 10.5 %all_to_all.31.parts = bf16[4,8,1664]{2,1,0:T(8,128)(2,1)S(1)} all-to-all(bf16[4,8,1664]{2,1,0:T(8,128)(2,1)S(1)} %shard_map.93), channel_id=1, replica_groups=mesh['x'=4,'yh'=4,'yl'=2,'zh'=4,'zl'=2,'c'=2] {'yh'}, dimensions={0} | all-to-all | bytes 212992 | tf_op jit(solution)/shard_map/all_to_all | solution.py:218
  69.4 1.0 shard_map.94
  70.4 3.5 %all-to-all-start.3 = ((bf16[8,32,1664]{2,1,0:T(8,128)(2,1)}), bf16[8,32,1664]{2,1,0:T(8,128)(2,1)S(1)}, u32[]{:S(2)}, u32[]{:S(2)}) async-start(bf16[8,32,1664]{2,1,0:T(8,128)(2,1)} %shard_map.94), calls=%async_computation.3 | async-start | bytes 1703936 | tf_op jit(solution)/shard_map/all_to_all | solution.py:218
  74.0 0.0 collective-permute-done.other_ref
  74.0 0.3 shard_map.96
  74.2 2.3 %collective-permute-start.1 = (bf16[416,256]{1,0:T(8,128)(2,1)S(1)}, bf16[416,256]{1,0:T(8,128)(2,1)S(1)}, u32[]{:S(2)}, u32[]{:S(2)}) collective-permute-start(bf16[416,256]{1,0:T(8,128)(2,1)S(1)} %get-tuple-element.13), channel_id=1, source_target_pairs={{0,4},{4,8},{8,12},{12,0},{1,5},{5,9},{9,13},{13,1},{2,6},{6,10},{... | collective-permute-start | bytes 638984 | tf_op jit(solution)/shard_map/ppermute | solution.py:262
  76.5 4.1 %collective-permute-start.2 = (bf16[416,256]{1,0:T(8,128)(2,1)S(1)}, bf16[416,256]{1,0:T(8,128)(2,1)S(1)}, u32[]{:S(2)}, u32[]{:S(2)}) collective-permute-start(bf16[416,256]{1,0:T(8,128)(2,1)S(1)} %get-tuple-element.14), channel_id=1, source_target_pairs={{0,8},{4,12},{8,0},{12,4},{1,9},{5,13},{9,1},{13,5},{2,10},{6,14},... | collective-permute-start | bytes 638984 | tf_op jit(solution)/shard_map/ppermute | solution.py:262
  80.7 4.3 %collective-permute-start.3 = (bf16[416,256]{1,0:T(8,128)(2,1)S(1)}, bf16[416,256]{1,0:T(8,128)(2,1)S(1)}, u32[]{:S(2)}, u32[]{:S(2)}) collective-permute-start(bf16[416,256]{1,0:T(8,128)(2,1)S(1)} %get-tuple-element.15), channel_id=1, source_target_pairs={{0,12},{4,0},{8,4},{12,8},{1,13},{5,1},{9,5},{13,9},{2,14},{6,2},{... | collective-permute-start | bytes 638984 | tf_op jit(solution)/shard_map/ppermute | solution.py:262
  85.0 0.5 collective-permute-done.1.refs_1_
  85.5 9.6 %collective-permute-done.2.refs_2_ = bf16[416,256]{1,0:T(8,128)(2,1)S(1)} collective-permute-done((bf16[416,256]{1,0:T(8,128)(2,1)S(1)}, bf16[416,256]{1,0:T(8,128)(2,1)S(1)}, u32[]{:S(2)}, u32[]{:S(2)}) %collective-permute-start.2) | collective-permute-done | bytes 213024 | tf_op jit(solution)/shard_map/ppermute | solution.py:262
  95.1 8.7 %collective-permute-done.3.refs_3_ = bf16[416,256]{1,0:T(8,128)(2,1)S(1)} collective-permute-done((bf16[416,256]{1,0:T(8,128)(2,1)S(1)}, bf16[416,256]{1,0:T(8,128)(2,1)S(1)}, u32[]{:S(2)}, u32[]{:S(2)}) %collective-permute-start.3) | collective-permute-done | bytes 213024 | tf_op jit(solution)/shard_map/ppermute | solution.py:262
  103.8 0.1 shard_map.97.own_ref
  103.8 1.9 %collective-permute-start.4 = (bf16[1664,256]{1,0:T(8,128)(2,1)S(1)}, bf16[1664,256]{1,0:T(8,128)(2,1)S(1)}, u32[]{:S(2)}, u32[]{:S(2)}) collective-permute-start(bf16[1664,256]{1,0:T(8,128)(2,1)S(1)} %shard_map.97.own_ref), channel_id=1, source_target_pairs={{0,2},{2,0},{1,3},{3,1},{4,6},{6,4},{5,7},{7,5},{8,10},{10,8},{9,1... | collective-permute-start | bytes 2555912 | tf_op jit(solution)/shard_map/ppermute | solution.py:226
  105.8 20.0 %collective-permute-done.4.other_ref = bf16[1664,256]{1,0:T(8,128)(2,1)S(1)} collective-permute-done((bf16[1664,256]{1,0:T(8,128)(2,1)S(1)}, bf16[1664,256]{1,0:T(8,128)(2,1)S(1)}, u32[]{:S(2)}, u32[]{:S(2)}) %collective-permute-start.4) | collective-permute-done | bytes 852000 | tf_op jit(solution)/shard_map/ppermute | solution.py:226
  125.8 0.0 all-to-all-done.3
  125.8 0.6 shard_map.98
  126.4 13.4 %all_to_all.32.parts = bf16[16,16,256]{2,1,0:T(8,128)(2,1)S(1)} all-to-all(bf16[16,16,256]{2,1,0:T(8,128)(2,1)S(1)} %bitcast.6), channel_id=1, replica_groups=mesh['x'=4,'yh'=4,'yl'=2,'zh'=4,'zl'=2,'c'=2] {'zh','zl','c'}, dimensions={0} | all-to-all | bytes 262144 | tf_op jit(solution)/shard_map/all_to_all | solution.py:218
  139.8 11.6 %all_to_all.33 = bf16[16,16,256]{2,1,0:T(8,128)(2,1)S(1)} all-to-all(bf16[16,16,256]{2,1,0:T(8,128)(2,1)S(1)} %shard_map.99), channel_id=1, replica_groups=mesh['x'=4,'yh'=4,'yl'=2,'zh'=4,'zl'=2,'c'=2] {'zh','zl','c'}, dimensions={0} | all-to-all | bytes 262144 | tf_op jit(solution)/shard_map/all_to_all | solution.py:218
  151.4 0.7 copy.11
  (1 shorter events, 0.0 us)
Async XLA Ops:
  28.9 17.9 %copy-start = (s32[832,256]{1,0:T(8,128)S(1)}, s32[832,256]{1,0:T(8,128)}, u32[]{:S(2)}) copy-start(s32[832,256]{1,0:T(8,128)} %codes.1) | copy-start | bytes 2555908
  28.9 17.9 %copy-start.1 = (bf16[13,256]{1,0:T(8,128)(2,1)S(1)}, bf16[13,256]{1,0:T(8,128)(2,1)}, u32[]{:S(2)}) copy-start(bf16[13,256]{1,0:T(8,128)(2,1)} %scales.1) | copy-start | bytes 19972
  29.9 28.7 %all-to-all-start.1 = ((bf16[16,8,896]{2,1,0:T(8,128)(2,1)}), bf16[16,8,896]{2,1,0:T(8,128)(2,1)S(1)}, u32[]{:S(2)}, u32[]{:S(2)}) async-start(bf16[16,8,896]{2,1,0:T(8,128)(2,1)} %shard_map.92), calls=%async_computation.1 | async-start | bytes 458752 | tf_op jit(solution)/shard_map/all_to_all | solution.py:218
  47.4 26.6 %collective-permute-start = (bf16[1664,256]{1,0:T(8,128)(2,1)S(1)}, bf16[1664,256]{1,0:T(8,128)(2,1)S(1)}, u32[]{:S(2)}, u32[]{:S(2)}) collective-permute-start(bf16[1664,256]{1,0:T(8,128)(2,1)S(1)} %shard_map.95.own_ref), channel_id=1, source_target_pairs={{0,1},{1,0},{2,3},{3,2},{4,5},{5,4},{6,7},{7,6},{8,9},{9,8},{10,11... | collective-permute-start | bytes 2555912 | tf_op jit(solution)/shard_map/ppermute | solution.py:226
  70.4 55.4 %all-to-all-start.3 = ((bf16[8,32,1664]{2,1,0:T(8,128)(2,1)}), bf16[8,32,1664]{2,1,0:T(8,128)(2,1)S(1)}, u32[]{:S(2)}, u32[]{:S(2)}) async-start(bf16[8,32,1664]{2,1,0:T(8,128)(2,1)} %shard_map.94), calls=%async_computation.3 | async-start | bytes 1703936 | tf_op jit(solution)/shard_map/all_to_all | solution.py:218
  74.2 11.3 %collective-permute-start.1 = (bf16[416,256]{1,0:T(8,128)(2,1)S(1)}, bf16[416,256]{1,0:T(8,128)(2,1)S(1)}, u32[]{:S(2)}, u32[]{:S(2)}) collective-permute-start(bf16[416,256]{1,0:T(8,128)(2,1)S(1)} %get-tuple-element.13), channel_id=1, source_target_pairs={{0,4},{4,8},{8,12},{12,0},{1,5},{5,9},{9,13},{13,1},{2,6},{6,10},{... | collective-permute-start | bytes 638984 | tf_op jit(solution)/shard_map/ppermute | solution.py:262
  76.5 18.5 %collective-permute-start.2 = (bf16[416,256]{1,0:T(8,128)(2,1)S(1)}, bf16[416,256]{1,0:T(8,128)(2,1)S(1)}, u32[]{:S(2)}, u32[]{:S(2)}) collective-permute-start(bf16[416,256]{1,0:T(8,128)(2,1)S(1)} %get-tuple-element.14), channel_id=1, source_target_pairs={{0,8},{4,12},{8,0},{12,4},{1,9},{5,13},{9,1},{13,5},{2,10},{6,14},... | collective-permute-start | bytes 638984 | tf_op jit(solution)/shard_map/ppermute | solution.py:262
  80.7 23.1 %collective-permute-start.3 = (bf16[416,256]{1,0:T(8,128)(2,1)S(1)}, bf16[416,256]{1,0:T(8,128)(2,1)S(1)}, u32[]{:S(2)}, u32[]{:S(2)}) collective-permute-start(bf16[416,256]{1,0:T(8,128)(2,1)S(1)} %get-tuple-element.15), channel_id=1, source_target_pairs={{0,12},{4,0},{8,4},{12,8},{1,13},{5,1},{9,5},{13,9},{2,14},{6,2},{... | collective-permute-start | bytes 638984 | tf_op jit(solution)/shard_map/ppermute | solution.py:262
  103.8 21.9 %collective-permute-start.4 = (bf16[1664,256]{1,0:T(8,128)(2,1)S(1)}, bf16[1664,256]{1,0:T(8,128)(2,1)S(1)}, u32[]{:S(2)}, u32[]{:S(2)}) collective-permute-start(bf16[1664,256]{1,0:T(8,128)(2,1)S(1)} %shard_map.97.own_ref), channel_id=1, source_target_pairs={{0,2},{2,0},{1,3},{3,1},{4,6},{6,4},{5,7},{7,5},{8,10},{10,8},{9,1... | collective-permute-start | bytes 2555912 | tf_op jit(solution)/shard_map/ppermute | solution.py:226

commit v5 on v4

--- a/solution.py
+++ b/solution.py
@@ -10,9 +10,10 @@
 ROWS = 256
 FACTOR = 128
 EPSILON = 1e-05
-NEAR = ("x", "yl")
-FAR = ("yh", "zh")
+NEAR = ("yl", "x")
+FAR = ("zh", "yh")
 TENSOR = ("zh", "zl", "c")
+SPREAD = ("c", "zh", "zl")
 N_NEAR = 8
 N_YH = 4
 N_ZH = 4
@@ -79,7 +80,7 @@
     order = (source == wanted).astype(F32).astype(BF16)
     words = gate_codes.shape[0]
     top = lax.broadcasted_iota(jnp.int32, (words, FACTOR), 0) < words // 2
-    my_t = (lax.axis_index("zh") * 2 + lax.axis_index("zl")) * 2 + lax.axis_index("c")
+    my_t = lax.axis_index(SPREAD)
     for copy in small:
         copy.wait()
     wide = x_ref[...].astype(F32)
@@ -151,7 +152,7 @@
         joined[:, 2 * SLICE : PIECE] = tail
         value = joined[...].astype(BF16)
         for yh in range(N_YH):
-            out_ref[yh * N_ZH + piece] = value[8 * yh : 8 * yh + 8, :]
+            out_ref[piece * N_YH + yh] = value[8 * yh : 8 * yh + 8, :]
 
 
 def source_of(shift):
@@ -162,9 +163,9 @@
     values = []
     inverse = None
     for z in range(N_ZH):
-        value = parts[z].astype(F32)
+        value = parts[z * N_YH].astype(F32)
         for yh in range(1, N_YH):
-            value = value + parts[yh * N_ZH + z].astype(F32)
+            value = value + parts[z * N_YH + yh].astype(F32)
         joined[...] = value
         if z == 0:
             squares = joined[:, 2 * SLICE : 2 * SLICE + 1] + joined[:, 2 * SLICE + 1 : 2 * SLICE + 2]
@@ -198,11 +199,12 @@
             out_ref[target, 8 * yh : 8 * yh + 8, :] = value
 
 
-def project_out(act_ref, own_ref, other_ref, out_ref):
-    act = act_ref[...]
-    own = jnp.dot(act, own_ref[...], preferred_element_type=F32)
-    other = jnp.dot(act, other_ref[...], preferred_element_type=F32)
-    out_ref[...] = (own * side("zl") + other).astype(BF16)
+def blend_chip(own_ref, other_ref, out_ref):
+    out_ref[...] = (own_ref[...].astype(F32) * side("zl") + other_ref[...].astype(F32)).astype(BF16)
+
+
+def project_out(act, weight, out_ref):
+    out_ref[...] = jnp.dot(act[...], weight[...], preferred_element_type=F32).astype(BF16)
 
 
 def finish(parts, residual, out_ref):
@@ -270,10 +272,11 @@
     back = exchange(mixed, "yh")
     copies = call(spread_near, shape((N_NEAR, NEAR_ROWS, LOCAL), BF16))(back)
     rotated = exchange(copies, NEAR).reshape(ROWS, LOCAL)
-    partial = call(project_out, shape((ROWS, columns), BF16), [])(rotated, weight, other)
-    sums = exchange(partial.reshape(N_T, OWN_ROWS, columns), TENSOR)
+    weight = call(blend_chip, shape((LOCAL, columns), BF16))(weight, other)
+    partial = call(project_out, shape((ROWS, columns), BF16))(rotated, weight)
+    sums = exchange(partial.reshape(N_T, OWN_ROWS, columns), SPREAD)
     out = call(finish, shape((N_T, OWN_ROWS, columns), BF16))(sums, own_rows)
-    return exchange(out, TENSOR).reshape(ROWS, columns)
+    return exchange(out, SPREAD).reshape(ROWS, columns)
 
 
 def solution(mesh):

time: 153 us -> 151 us (0.987)
  transfers between devices with their start and end apart: 7 -> 7, of which waited for: 5 -> 5; matrix products, arithmetic and copies ran while one was open for 0% -> 0% of each run, Pallas kernels for 1% -> 2%
where the time goes in v5:
time: 151 us
  blocking collectives  60.5 us (40%)
  waiting for transfers between devices  44.3 us (29%)
  starting transfers between devices  37.8 us (25%)
  Pallas kernels  7.05 us (5%)
    all_to_all x4, blocking collectives, exchange(): return lax.all_to_all(blocks, axes, split_axis=0, concat_axis=0, tiled=True)  60.5 us
    all_to_all x2, starting transfers between devices, exchange(): return lax.all_to_all(blocks, axes, split_axis=0, concat_axis=0, tiled=True)  20.7 us
    ppermute x2, waiting for transfers between devices, swapped(): return lax.ppermute(weight, axis, [(0, 1), (1, 0)])  19.5 us
    ppermute x3, waiting for transfers between devices, shards(): lax.ppermute(groups[j], 'zh', [(i, (i + j) % N_ZH) for i in range(N_ZH)])  17.9 us
    ppermute x3, starting transfers between devices, shards(): lax.ppermute(groups[j], 'zh', [(i, (i + j) % N_ZH) for i in range(N_ZH)])  10.7 us
    all_to_all x2, waiting for transfers between devices, exchange(): return lax.all_to_all(blocks, axes, split_axis=0, concat_axis=0, tiled=True)  6.93 us
    ppermute x2, starting transfers between devices, swapped(): return lax.ppermute(weight, axis, [(0, 1), (1, 0)])  6.43 us
    pallas_call x1, Pallas kernels, shards(): pl.pallas_call(project_in, out_shape=[shape((ROWS, WIDE), BF16), shape((O...  3.16 us
  transfers between devices with their start and end apart: 7, of which 5 were waited for; matrix products, arithmetic and copies ran while one was open for 0% of the time, Pallas kernels for 2%

profile of v5, /device:TPU:1, one launch (start us, length us, event | category | flops | bytes accessed | tf_op | source)
XLA Modules:
  0.0 150.5 jit_solution(11137173964845657376)
XLA Ops:
  0.0 3.2 %shard_map.91 = (bf16[256,3456]{1,0:T(8,128)(2,1)S(1)}, bf16[16,256]{1,0:T(8,128)(2,1)S(1)}) custom-call(bf16[256,256]{1,0:T(8,128)(2,1)} %x_hbm.1, bf16[256]{0:T(256)(128)(2,1)} %gain_hbm.1, s32[128,1664]{1,0:T(8,128)} %gate_hbm.1, bf16[2,1664]{1,0:T(2,128)(2,1)} %gate_scales_hbm.1, s32[128,1664]{1,0:T(8,128)} %up_hbm.1, bf16[2,1664]{1,0:T(2,128)(2,1)} %up_scales_hbm.1, ...), custom_call_target="tpu_custom_call" | custom-call | tf_op jit(solution)/shard_map/pallas_call | solution.py:249
  3.2 25.3 %all_to_all.30.parts = bf16[8,32,3456]{2,1,0:T(8,128)(2,1)S(1)} all-to-all(bf16[8,32,3456]{2,1,0:T(8,128)(2,1)S(1)} %bitcast.5), channel_id=1, replica_groups=mesh['x'=4,'yh'=4,'yl'=2,'zh'=4,'zl'=2,'c'=2] {'yl','x'}, dimensions={0} | all-to-all | bytes 3538944 | tf_op jit(solution)/shard_map/all_to_all | solution.py:220
  28.5 0.0 copy-start
  28.5 0.0 copy-start.1
  28.5 1.0 shard_map.92
  29.5 17.2 %all-to-all-start.1 = ((bf16[16,8,896]{2,1,0:T(8,128)(2,1)}), bf16[16,8,896]{2,1,0:T(8,128)(2,1)S(1)}, u32[]{:S(2)}, u32[]{:S(2)}) async-start(bf16[16,8,896]{2,1,0:T(8,128)(2,1)} %shard_map.92), calls=%async_computation.1 | async-start | bytes 458752 | tf_op jit(solution)/shard_map/all_to_all | solution.py:220
  46.7 0.0 copy-done
  46.7 0.0 copy-done.1
  46.7 0.5 shard_map.95.own_ref
  47.2 4.5 %collective-permute-start = (bf16[1664,256]{1,0:T(8,128)(2,1)S(1)}, bf16[1664,256]{1,0:T(8,128)(2,1)S(1)}, u32[]{:S(2)}, u32[]{:S(2)}) collective-permute-start(bf16[1664,256]{1,0:T(8,128)(2,1)S(1)} %shard_map.95.own_ref), channel_id=1, source_target_pairs={{0,1},{1,0},{2,3},{3,2},{4,5},{5,4},{6,7},{7,6},{8,9},{9,8},{10,11... | collective-permute-start | bytes 2555912 | tf_op jit(solution)/shard_map/ppermute | solution.py:228
  51.7 6.9 %all-to-all-done.1.parts = bf16[16,8,896]{2,1,0:T(8,128)(2,1)S(1)} async-done(((bf16[16,8,896]{2,1,0:T(8,128)(2,1)}), bf16[16,8,896]{2,1,0:T(8,128)(2,1)S(1)}, u32[]{:S(2)}, u32[]{:S(2)}) %all-to-all-start.1) | async-done | bytes 229408 | tf_op jit(solution)/shard_map/all_to_all | solution.py:220
  58.7 0.3 shard_map.93
  59.0 10.5 %all_to_all.31.parts = bf16[4,8,1664]{2,1,0:T(8,128)(2,1)S(1)} all-to-all(bf16[4,8,1664]{2,1,0:T(8,128)(2,1)S(1)} %shard_map.93), channel_id=1, replica_groups=mesh['x'=4,'yh'=4,'yl'=2,'zh'=4,'zl'=2,'c'=2] {'yh'}, dimensions={0} | all-to-all | bytes 212992 | tf_op jit(solution)/shard_map/all_to_all | solution.py:220
  69.5 1.0 shard_map.94
  70.5 3.5 %all-to-all-start.3 = ((bf16[8,32,1664]{2,1,0:T(8,128)(2,1)}), bf16[8,32,1664]{2,1,0:T(8,128)(2,1)S(1)}, u32[]{:S(2)}, u32[]{:S(2)}) async-start(bf16[8,32,1664]{2,1,0:T(8,128)(2,1)} %shard_map.94), calls=%async_computation.3 | async-start | bytes 1703936 | tf_op jit(solution)/shard_map/all_to_all | solution.py:220
  74.0 0.0 collective-permute-done.other_ref
  74.1 0.3 shard_map.96
  74.3 1.9 %collective-permute-start.1 = (bf16[416,256]{1,0:T(8,128)(2,1)S(1)}, bf16[416,256]{1,0:T(8,128)(2,1)S(1)}, u32[]{:S(2)}, u32[]{:S(2)}) collective-permute-start(bf16[416,256]{1,0:T(8,128)(2,1)S(1)} %get-tuple-element.13), channel_id=1, source_target_pairs={{0,4},{4,8},{8,12},{12,0},{1,5},{5,9},{9,13},{13,1},{2,6},{6,10},{... | collective-permute-start | bytes 638984 | tf_op jit(solution)/shard_map/ppermute | solution.py:264
  76.3 4.5 %collective-permute-start.2 = (bf16[416,256]{1,0:T(8,128)(2,1)S(1)}, bf16[416,256]{1,0:T(8,128)(2,1)S(1)}, u32[]{:S(2)}, u32[]{:S(2)}) collective-permute-start(bf16[416,256]{1,0:T(8,128)(2,1)S(1)} %get-tuple-element.14), channel_id=1, source_target_pairs={{0,8},{4,12},{8,0},{12,4},{1,9},{5,13},{9,1},{13,5},{2,10},{6,14},... | collective-permute-start | bytes 638984 | tf_op jit(solution)/shard_map/ppermute | solution.py:264
  80.8 4.3 %collective-permute-start.3 = (bf16[416,256]{1,0:T(8,128)(2,1)S(1)}, bf16[416,256]{1,0:T(8,128)(2,1)S(1)}, u32[]{:S(2)}, u32[]{:S(2)}) collective-permute-start(bf16[416,256]{1,0:T(8,128)(2,1)S(1)} %get-tuple-element.15), channel_id=1, source_target_pairs={{0,12},{4,0},{8,4},{12,8},{1,13},{5,1},{9,5},{13,9},{2,14},{6,2},{... | collective-permute-start | bytes 638984 | tf_op jit(solution)/shard_map/ppermute | solution.py:264
  85.0 3.9 %collective-permute-done.1.refs_1_ = bf16[416,256]{1,0:T(8,128)(2,1)S(1)} collective-permute-done((bf16[416,256]{1,0:T(8,128)(2,1)S(1)}, bf16[416,256]{1,0:T(8,128)(2,1)S(1)}, u32[]{:S(2)}, u32[]{:S(2)}) %collective-permute-start.1) | collective-permute-done | bytes 213024 | tf_op jit(solution)/shard_map/ppermute | solution.py:264
  88.9 5.5 %collective-permute-done.2.refs_2_ = bf16[416,256]{1,0:T(8,128)(2,1)S(1)} collective-permute-done((bf16[416,256]{1,0:T(8,128)(2,1)S(1)}, bf16[416,256]{1,0:T(8,128)(2,1)S(1)}, u32[]{:S(2)}, u32[]{:S(2)}) %collective-permute-start.2) | collective-permute-done | bytes 213024 | tf_op jit(solution)/shard_map/ppermute | solution.py:264
  94.4 8.5 %collective-permute-done.3.refs_3_ = bf16[416,256]{1,0:T(8,128)(2,1)S(1)} collective-permute-done((bf16[416,256]{1,0:T(8,128)(2,1)S(1)}, bf16[416,256]{1,0:T(8,128)(2,1)S(1)}, u32[]{:S(2)}, u32[]{:S(2)}) %collective-permute-start.3) | collective-permute-done | bytes 213024 | tf_op jit(solution)/shard_map/ppermute | solution.py:264
  102.9 0.1 shard_map.97.own_ref
  103.0 1.9 %collective-permute-start.4 = (bf16[1664,256]{1,0:T(8,128)(2,1)S(1)}, bf16[1664,256]{1,0:T(8,128)(2,1)S(1)}, u32[]{:S(2)}, u32[]{:S(2)}) collective-permute-start(bf16[1664,256]{1,0:T(8,128)(2,1)S(1)} %shard_map.97.own_ref), channel_id=1, source_target_pairs={{0,2},{2,0},{1,3},{3,1},{4,6},{6,4},{5,7},{7,5},{8,10},{10,8},{9,1... | collective-permute-start | bytes 2555912 | tf_op jit(solution)/shard_map/ppermute | solution.py:228
  104.9 19.5 %collective-permute-done.4.other_ref = bf16[1664,256]{1,0:T(8,128)(2,1)S(1)} collective-permute-done((bf16[1664,256]{1,0:T(8,128)(2,1)S(1)}, bf16[1664,256]{1,0:T(8,128)(2,1)S(1)}, u32[]{:S(2)}, u32[]{:S(2)}) %collective-permute-start.4) | collective-permute-done | bytes 852000 | tf_op jit(solution)/shard_map/ppermute | solution.py:228
  124.4 0.3 shard_map.98.weight
  124.7 0.0 all-to-all-done.3
  124.7 0.4 shard_map.99
  125.1 13.2 %all_to_all.32.parts = bf16[16,16,256]{2,1,0:T(8,128)(2,1)S(1)} all-to-all(bf16[16,16,256]{2,1,0:T(8,128)(2,1)S(1)} %bitcast.6), channel_id=1, replica_groups=mesh['x'=4,'yh'=4,'yl'=2,'zh'=4,'zl'=2,'c'=2] {'c','zh','zl'}, dimensions={0} | all-to-all | bytes 262144 | tf_op jit(solution)/shard_map/all_to_all | solution.py:220
  138.3 11.6 %all_to_all.33 = bf16[16,16,256]{2,1,0:T(8,128)(2,1)S(1)} all-to-all(bf16[16,16,256]{2,1,0:T(8,128)(2,1)S(1)} %shard_map.100), channel_id=1, replica_groups=mesh['x'=4,'yh'=4,'yl'=2,'zh'=4,'zl'=2,'c'=2] {'c','zh','zl'}, dimensions={0} | all-to-all | bytes 262144 | tf_op jit(solution)/shard_map/all_to_all | solution.py:220
  149.9 0.7 copy.11
  (1 shorter events, 0.0 us)
Async XLA Ops:
  28.5 18.2 %copy-start = (s32[832,256]{1,0:T(8,128)S(1)}, s32[832,256]{1,0:T(8,128)}, u32[]{:S(2)}) copy-start(s32[832,256]{1,0:T(8,128)} %codes.1) | copy-start | bytes 2555908
  28.5 18.2 %copy-start.1 = (bf16[13,256]{1,0:T(8,128)(2,1)S(1)}, bf16[13,256]{1,0:T(8,128)(2,1)}, u32[]{:S(2)}) copy-start(bf16[13,256]{1,0:T(8,128)(2,1)} %scales.1) | copy-start | bytes 19972
  29.5 29.2 %all-to-all-start.1 = ((bf16[16,8,896]{2,1,0:T(8,128)(2,1)}), bf16[16,8,896]{2,1,0:T(8,128)(2,1)S(1)}, u32[]{:S(2)}, u32[]{:S(2)}) async-start(bf16[16,8,896]{2,1,0:T(8,128)(2,1)} %shard_map.92), calls=%async_computation.1 | async-start | bytes 458752 | tf_op jit(solution)/shard_map/all_to_all | solution.py:220
  47.2 26.8 %collective-permute-start = (bf16[1664,256]{1,0:T(8,128)(2,1)S(1)}, bf16[1664,256]{1,0:T(8,128)(2,1)S(1)}, u32[]{:S(2)}, u32[]{:S(2)}) collective-permute-start(bf16[1664,256]{1,0:T(8,128)(2,1)S(1)} %shard_map.95.own_ref), channel_id=1, source_target_pairs={{0,1},{1,0},{2,3},{3,2},{4,5},{5,4},{6,7},{7,6},{8,9},{9,8},{10,11... | collective-permute-start | bytes 2555912 | tf_op jit(solution)/shard_map/ppermute | solution.py:228
  70.5 54.2 %all-to-all-start.3 = ((bf16[8,32,1664]{2,1,0:T(8,128)(2,1)}), bf16[8,32,1664]{2,1,0:T(8,128)(2,1)S(1)}, u32[]{:S(2)}, u32[]{:S(2)}) async-start(bf16[8,32,1664]{2,1,0:T(8,128)(2,1)} %shard_map.94), calls=%async_computation.3 | async-start | bytes 1703936 | tf_op jit(solution)/shard_map/all_to_all | solution.py:220
  74.3 14.6 %collective-permute-start.1 = (bf16[416,256]{1,0:T(8,128)(2,1)S(1)}, bf16[416,256]{1,0:T(8,128)(2,1)S(1)}, u32[]{:S(2)}, u32[]{:S(2)}) collective-permute-start(bf16[416,256]{1,0:T(8,128)(2,1)S(1)} %get-tuple-element.13), channel_id=1, source_target_pairs={{0,4},{4,8},{8,12},{12,0},{1,5},{5,9},{9,13},{13,1},{2,6},{6,10},{... | collective-permute-start | bytes 638984 | tf_op jit(solution)/shard_map/ppermute | solution.py:264
  76.3 18.2 %collective-permute-start.2 = (bf16[416,256]{1,0:T(8,128)(2,1)S(1)}, bf16[416,256]{1,0:T(8,128)(2,1)S(1)}, u32[]{:S(2)}, u32[]{:S(2)}) collective-permute-start(bf16[416,256]{1,0:T(8,128)(2,1)S(1)} %get-tuple-element.14), channel_id=1, source_target_pairs={{0,8},{4,12},{8,0},{12,4},{1,9},{5,13},{9,1},{13,5},{2,10},{6,14},... | collective-permute-start | bytes 638984 | tf_op jit(solution)/shard_map/ppermute | solution.py:264
  80.8 22.2 %collective-permute-start.3 = (bf16[416,256]{1,0:T(8,128)(2,1)S(1)}, bf16[416,256]{1,0:T(8,128)(2,1)S(1)}, u32[]{:S(2)}, u32[]{:S(2)}) collective-permute-start(bf16[416,256]{1,0:T(8,128)(2,1)S(1)} %get-tuple-element.15), channel_id=1, source_target_pairs={{0,12},{4,0},{8,4},{12,8},{1,13},{5,1},{9,5},{13,9},{2,14},{6,2},{... | collective-permute-start | bytes 638984 | tf_op jit(solution)/shard_map/ppermute | solution.py:264
  103.0 21.4 %collective-permute-start.4 = (bf16[1664,256]{1,0:T(8,128)(2,1)S(1)}, bf16[1664,256]{1,0:T(8,128)(2,1)S(1)}, u32[]{:S(2)}, u32[]{:S(2)}) collective-permute-start(bf16[1664,256]{1,0:T(8,128)(2,1)S(1)} %shard_map.97.own_ref), channel_id=1, source_target_pairs={{0,2},{2,0},{1,3},{3,1},{4,6},{6,4},{5,7},{7,5},{8,10},{10,8},{9,1... | collective-permute-start | bytes 2555912 | tf_op jit(solution)/shard_map/ppermute | solution.py:228

commit v6 on v5

--- a/solution.py
+++ b/solution.py
@@ -21,7 +21,7 @@
 LOCAL = 1664
 SLICE = LOCAL // N_ZH
 BLOCKS = LOCAL // FACTOR
-WIDE = 2 * LOCAL + 128
+TILES = 4 * (2 * LOCAL // 128) + 1
 PIECE = 2 * SLICE + 64
 NEAR_ROWS = ROWS // N_NEAR
 OWN_ROWS = ROWS // N_T
@@ -87,15 +87,21 @@
     scaled = (wide * gain_ref[...].reshape(1, width).astype(F32)).astype(BF16)
     ordered = jnp.dot(scaled, order, preferred_element_type=F32).astype(BF16)
     squares = jnp.sum(wide * wide, axis=1, keepdims=True)
-    out_ref[:, pl.ds(2 * LOCAL, 128)] = two_parts(squares, 128).astype(BF16)
+    coarse = squares.astype(BF16).astype(F32)
+    both = [jnp.broadcast_to(value, (ROWS, 128)).reshape(N_NEAR, 4, 8, 128) for value in (coarse, squares - coarse)]
+    lane = lax.broadcasted_iota(jnp.int32, (N_NEAR, 8, 128), 2)
+    tile = jnp.zeros((N_NEAR, 8, 128), F32)
+    for place in range(8):
+        tile = jnp.where(lane == place, both[place % 2][:, place // 2], tile)
+    out_ref[:, TILES - 1] = tile.astype(BF16)
     leaving = []
 
     def leave(first, width):
-        lanes = pl.ds(first, width)
-        leaving.append(pltpu.make_async_copy(out_ref.at[:, lanes], out_hbm.at[:, lanes], out_sems.at[len(leaving)]))
+        tiles = pl.ds(first, width)
+        leaving.append(pltpu.make_async_copy(out_ref.at[:, tiles], out_hbm.at[:, tiles], out_sems.at[len(leaving)]))
         leaving[-1].start()
 
-    leave(2 * LOCAL, 128)
+    leave(TILES - 1, 1)
     own_ref[...] = x_ref[pl.ds(pl.multiple_of(my_t * OWN_ROWS, OWN_ROWS), OWN_ROWS), :]
 
     for which, (codes, scales, base) in enumerate(((gate_codes, gate_scales, 0), (up_codes, up_scales, LOCAL))):
@@ -112,10 +118,11 @@
             high = (((word >> 4) - 8).astype(F32) * spread).astype(BF16)
             weight = jnp.concatenate([low, high], axis=0)
             part = jnp.dot(ordered, weight, preferred_element_type=F32)
-            out_ref[:, pl.ds(base + block * FACTOR, FACTOR)] = part.astype(BF16)
+            column = base // FACTOR + block
+            out_ref[:, pl.ds(4 * column, 4)] = part.reshape(N_NEAR, 4, 8, 128).astype(BF16)
             if block + 1 in ends:
                 first = ends[ends.index(block + 1) - 1]
-                leave(base + first * FACTOR, (block + 1 - first) * FACTOR)
+                leave(4 * (base // FACTOR + first), 4 * (block + 1 - first))
     for copy in leaving:
         copy.wait()
 
@@ -138,13 +145,16 @@
 
 
 def sum_near(parts, out_ref, total, joined):
-    for block in range(WIDE // 128):
-        lanes = pl.ds(block * 128, 128)
-        value = parts[0, :, lanes].astype(F32)
+    def summed(first, width):
+        value = parts[0, first : first + width].astype(F32)
         for source in range(1, N_NEAR):
-            value = value + parts[source, :, lanes].astype(F32)
-        total[:, lanes] = value
-    squares = total[:, pl.ds(2 * LOCAL, 1)] + total[:, pl.ds(2 * LOCAL + 1, 1)]
+            value = value + parts[source, first : first + width].astype(F32)
+        return value
+
+    for column in range(2 * BLOCKS):
+        total[:, column * 128 : (column + 1) * 128] = summed(4 * column, 4).reshape(NEAR_ROWS, 128)
+    tile = summed(TILES - 1, 1).reshape(8, 128)
+    squares = jnp.concatenate([tile[:, 2 * i : 2 * i + 1] + tile[:, 2 * i + 1 : 2 * i + 2] for i in range(4)], axis=0)
     tail = two_parts(squares, 64)
     for piece in range(N_ZH):
         joined[:, 0:SLICE] = total[:, piece * SLICE : (piece + 1) * SLICE]
@@ -248,14 +258,14 @@
     inputs = (residual, norm_gain, gate_codes, gate_scales, up_codes, up_scales, hidden_signs)
     part, own_rows = pl.pallas_call(
         project_in,
-        out_shape=[shape((ROWS, WIDE), BF16), shape((OWN_ROWS, columns), BF16)],
+        out_shape=[shape((N_NEAR, TILES, 8, 128), BF16), shape((OWN_ROWS, columns), BF16)],
         in_specs=[pl.BlockSpec(memory_space=pltpu.HBM)] * len(inputs),
         out_specs=[pl.BlockSpec(memory_space=pltpu.HBM), pl.BlockSpec(memory_space=pltpu.VMEM)],
-        scratch_shapes=[pltpu.VMEM((ROWS, WIDE), BF16), pltpu.SemaphoreType.DMA((5,))]
+        scratch_shapes=[pltpu.VMEM((N_NEAR, TILES, 8, 128), BF16), pltpu.SemaphoreType.DMA((5,))]
         + [pltpu.VMEM(a.shape, a.dtype) for a in inputs] + [pltpu.SemaphoreType.DMA((7,))],
         compiler_params=pltpu.CompilerParams(vmem_limit_bytes=48 << 20),
     )(*(pltpu.with_memory_space_constraint(a, pltpu.HBM) for a in inputs))
-    near = exchange(part.reshape(N_NEAR, NEAR_ROWS, WIDE), NEAR)
+    near = exchange(part, NEAR)
     weight = call(rotate_down, shape((LOCAL, columns), BF16))(down_codes, down_scales)
     other = swapped(weight, "c")
     groups = call(blend_core, [shape((SLICE, columns), BF16)] * N_ZH)(weight, other)
@@ -264,7 +274,7 @@
         dealt.append(lax.ppermute(groups[j], "zh", [(i, (i + j) % N_ZH) for i in range(N_ZH)]))
     weight = call(join, shape((LOCAL, columns), BF16))(*dealt)
     other = swapped(weight, "zl")
-    scratch = [pltpu.VMEM((NEAR_ROWS, WIDE), F32), pltpu.VMEM((NEAR_ROWS, PIECE), F32)]
+    scratch = [pltpu.VMEM((NEAR_ROWS, 2 * LOCAL), F32), pltpu.VMEM((NEAR_ROWS, PIECE), F32)]
     pieces = call(sum_near, shape((N_YH * N_ZH, 8, PIECE), BF16), scratch)(near)
     far = exchange(pieces, FAR)
     scratch = [pltpu.VMEM((8, PIECE), F32), pltpu.VMEM((N_ZH, 8, SLICE), F32), pltpu.VMEM((8, LOCAL), F32)]

time: 151 us -> 150 us (level)
  transfers between devices with their start and end apart: 7 -> 7, of which waited for: 5 -> 4; matrix products, arithmetic and copies ran while one was open for 0% -> 0% of each run, Pallas kernels for 2% -> 2%
where the time goes in v6:
time: 150 us
  blocking collectives  60.2 us (40%)
  waiting for transfers between devices  43.7 us (29%)
  starting transfers between devices  37.9 us (25%)
  Pallas kernels  7.08 us (5%)
    all_to_all x4, blocking collectives, exchange(): return lax.all_to_all(blocks, axes, split_axis=0, concat_axis=0, tiled=True)  60.2 us
    all_to_all x2, starting transfers between devices, exchange(): return lax.all_to_all(blocks, axes, split_axis=0, concat_axis=0, tiled=True)  20.8 us
    ppermute x2, waiting for transfers between devices, swapped(): return lax.ppermute(weight, axis, [(0, 1), (1, 0)])  19.1 us
    ppermute x3, waiting for transfers between devices, shards(): lax.ppermute(groups[j], 'zh', [(i, (i + j) % N_ZH) for i in range(N_ZH)])  17.5 us
    ppermute x3, starting transfers between devices, shards(): lax.ppermute(groups[j], 'zh', [(i, (i + j) % N_ZH) for i in range(N_ZH)])  10.8 us
    all_to_all x2, waiting for transfers between devices, exchange(): return lax.all_to_all(blocks, axes, split_axis=0, concat_axis=0, tiled=True)  7.04 us
    ppermute x2, starting transfers between devices, swapped(): return lax.ppermute(weight, axis, [(0, 1), (1, 0)])  6.3 us
    pallas_call x1, Pallas kernels, shards(): pl.pallas_call(project_in, out_shape=[shape((N_NEAR, TILES, 8, 128), BF16...  3.2 us
  transfers between devices with their start and end apart: 7, of which 4 were waited for; matrix products, arithmetic and copies ran while one was open for 0% of the time, Pallas kernels for 2%

profile of v6, /device:TPU:1, one launch (start us, length us, event | category | flops | bytes accessed | tf_op | source)
XLA Modules:
  0.0 149.7 jit_solution(13611670135407752997)
XLA Ops:
  0.0 3.2 %shard_map.91 = (bf16[8,105,8,128]{3,2,1,0:T(8,128)(2,1)S(1)}, bf16[16,256]{1,0:T(8,128)(2,1)S(1)}) custom-call(bf16[256,256]{1,0:T(8,128)(2,1)} %x_hbm.1, bf16[256]{0:T(256)(128)(2,1)} %gain_hbm.1, s32[128,1664]{1,0:T(8,128)} %gate_hbm.1, bf16[2,1664]{1,0:T(2,128)(2,1)} %gate_scales_hbm.1, s32[128,1664]{1,0:T(8,128)} %up_hbm.1, ...), custom_call_target="tpu_custom_call" | custom-call | tf_op jit(solution)/shard_map/pallas_call | solution.py:259
  3.2 24.8 %all_to_all.30.parts = bf16[8,105,8,128]{3,2,1,0:T(8,128)(2,1)S(1)} all-to-all(bf16[8,105,8,128]{3,2,1,0:T(8,128)(2,1)S(1)} %get-tuple-element.11), channel_id=1, replica_groups=mesh['x'=4,'yh'=4,'yl'=2,'zh'=4,'zl'=2,'c'=2] {'yl','x'}, dimensions={0} | all-to-all | bytes 3440640 | tf_op jit(solution)/shard_map/all_to_all | solution.py:230
  28.0 0.0 copy-start
  28.0 0.0 copy-start.1
  28.0 1.0 shard_map.92
  29.0 17.3 %all-to-all-start.1 = ((bf16[16,8,896]{2,1,0:T(8,128)(2,1)}), bf16[16,8,896]{2,1,0:T(8,128)(2,1)S(1)}, u32[]{:S(2)}, u32[]{:S(2)}) async-start(bf16[16,8,896]{2,1,0:T(8,128)(2,1)} %shard_map.92), calls=%async_computation.1 | async-start | bytes 458752 | tf_op jit(solution)/shard_map/all_to_all | solution.py:230
  46.3 0.0 copy-done
  46.3 0.0 copy-done.1
  46.3 0.5 shard_map.95.own_ref
  46.8 4.4 %collective-permute-start = (bf16[1664,256]{1,0:T(8,128)(2,1)S(1)}, bf16[1664,256]{1,0:T(8,128)(2,1)S(1)}, u32[]{:S(2)}, u32[]{:S(2)}) collective-permute-start(bf16[1664,256]{1,0:T(8,128)(2,1)S(1)} %shard_map.95.own_ref), channel_id=1, source_target_pairs={{0,1},{1,0},{2,3},{3,2},{4,5},{5,4},{6,7},{7,6},{8,9},{9,8},{10,11... | collective-permute-start | bytes 2555912 | tf_op jit(solution)/shard_map/ppermute | solution.py:238
  51.2 7.0 %all-to-all-done.1.parts = bf16[16,8,896]{2,1,0:T(8,128)(2,1)S(1)} async-done(((bf16[16,8,896]{2,1,0:T(8,128)(2,1)}), bf16[16,8,896]{2,1,0:T(8,128)(2,1)S(1)}, u32[]{:S(2)}, u32[]{:S(2)}) %all-to-all-start.1) | async-done | bytes 229408 | tf_op jit(solution)/shard_map/all_to_all | solution.py:230
  58.3 0.3 shard_map.93
  58.6 10.3 %all_to_all.31.parts = bf16[4,8,1664]{2,1,0:T(8,128)(2,1)S(1)} all-to-all(bf16[4,8,1664]{2,1,0:T(8,128)(2,1)S(1)} %shard_map.93), channel_id=1, replica_groups=mesh['x'=4,'yh'=4,'yl'=2,'zh'=4,'zl'=2,'c'=2] {'yh'}, dimensions={0} | all-to-all | bytes 212992 | tf_op jit(solution)/shard_map/all_to_all | solution.py:230
  68.9 1.0 shard_map.94
  69.9 3.5 %all-to-all-start.3 = ((bf16[8,32,1664]{2,1,0:T(8,128)(2,1)}), bf16[8,32,1664]{2,1,0:T(8,128)(2,1)S(1)}, u32[]{:S(2)}, u32[]{:S(2)}) async-start(bf16[8,32,1664]{2,1,0:T(8,128)(2,1)} %shard_map.94), calls=%async_computation.3 | async-start | bytes 1703936 | tf_op jit(solution)/shard_map/all_to_all | solution.py:230
  73.4 0.0 collective-permute-done.other_ref
  73.4 0.3 shard_map.96
  73.7 1.9 %collective-permute-start.1 = (bf16[416,256]{1,0:T(8,128)(2,1)S(1)}, bf16[416,256]{1,0:T(8,128)(2,1)S(1)}, u32[]{:S(2)}, u32[]{:S(2)}) collective-permute-start(bf16[416,256]{1,0:T(8,128)(2,1)S(1)} %get-tuple-element.13), channel_id=1, source_target_pairs={{0,4},{4,8},{8,12},{12,0},{1,5},{5,9},{9,13},{13,1},{2,6},{6,10},{... | collective-permute-start | bytes 638984 | tf_op jit(solution)/shard_map/ppermute | solution.py:274
  75.6 5.7 %collective-permute-start.2 = (bf16[416,256]{1,0:T(8,128)(2,1)S(1)}, bf16[416,256]{1,0:T(8,128)(2,1)S(1)}, u32[]{:S(2)}, u32[]{:S(2)}) collective-permute-start(bf16[416,256]{1,0:T(8,128)(2,1)S(1)} %get-tuple-element.14), channel_id=1, source_target_pairs={{0,8},{4,12},{8,0},{12,4},{1,9},{5,13},{9,1},{13,5},{2,10},{6,14},... | collective-permute-start | bytes 638984 | tf_op jit(solution)/shard_map/ppermute | solution.py:274
  81.3 3.2 %collective-permute-start.3 = (bf16[416,256]{1,0:T(8,128)(2,1)S(1)}, bf16[416,256]{1,0:T(8,128)(2,1)S(1)}, u32[]{:S(2)}, u32[]{:S(2)}) collective-permute-start(bf16[416,256]{1,0:T(8,128)(2,1)S(1)} %get-tuple-element.15), channel_id=1, source_target_pairs={{0,12},{4,0},{8,4},{12,8},{1,13},{5,1},{9,5},{13,9},{2,14},{6,2},{... | collective-permute-start | bytes 638984 | tf_op jit(solution)/shard_map/ppermute | solution.py:274
  84.5 0.0 collective-permute-done.1.refs_1_
  84.5 12.1 %collective-permute-done.2.refs_2_ = bf16[416,256]{1,0:T(8,128)(2,1)S(1)} collective-permute-done((bf16[416,256]{1,0:T(8,128)(2,1)S(1)}, bf16[416,256]{1,0:T(8,128)(2,1)S(1)}, u32[]{:S(2)}, u32[]{:S(2)}) %collective-permute-start.2) | collective-permute-done | bytes 213024 | tf_op jit(solution)/shard_map/ppermute | solution.py:274
  96.6 5.5 %collective-permute-done.3.refs_3_ = bf16[416,256]{1,0:T(8,128)(2,1)S(1)} collective-permute-done((bf16[416,256]{1,0:T(8,128)(2,1)S(1)}, bf16[416,256]{1,0:T(8,128)(2,1)S(1)}, u32[]{:S(2)}, u32[]{:S(2)}) %collective-permute-start.3) | collective-permute-done | bytes 213024 | tf_op jit(solution)/shard_map/ppermute | solution.py:274
  102.1 0.1 shard_map.97.own_ref
  102.1 1.9 %collective-permute-start.4 = (bf16[1664,256]{1,0:T(8,128)(2,1)S(1)}, bf16[1664,256]{1,0:T(8,128)(2,1)S(1)}, u32[]{:S(2)}, u32[]{:S(2)}) collective-permute-start(bf16[1664,256]{1,0:T(8,128)(2,1)S(1)} %shard_map.97.own_ref), channel_id=1, source_target_pairs={{0,2},{2,0},{1,3},{3,1},{4,6},{6,4},{5,7},{7,5},{8,10},{10,8},{9,1... | collective-permute-start | bytes 2555912 | tf_op jit(solution)/shard_map/ppermute | solution.py:238
  104.1 19.1 %collective-permute-done.4.other_ref = bf16[1664,256]{1,0:T(8,128)(2,1)S(1)} collective-permute-done((bf16[1664,256]{1,0:T(8,128)(2,1)S(1)}, bf16[1664,256]{1,0:T(8,128)(2,1)S(1)}, u32[]{:S(2)}, u32[]{:S(2)}) %collective-permute-start.4) | collective-permute-done | bytes 852000 | tf_op jit(solution)/shard_map/ppermute | solution.py:238
  123.2 0.3 shard_map.98.weight
  123.4 0.0 all-to-all-done.3
  123.4 0.4 shard_map.99
  123.8 13.6 %all_to_all.32.parts = bf16[16,16,256]{2,1,0:T(8,128)(2,1)S(1)} all-to-all(bf16[16,16,256]{2,1,0:T(8,128)(2,1)S(1)} %bitcast.4), channel_id=1, replica_groups=mesh['x'=4,'yh'=4,'yl'=2,'zh'=4,'zl'=2,'c'=2] {'c','zh','zl'}, dimensions={0} | all-to-all | bytes 262144 | tf_op jit(solution)/shard_map/all_to_all | solution.py:230
  137.4 11.6 %all_to_all.33 = bf16[16,16,256]{2,1,0:T(8,128)(2,1)S(1)} all-to-all(bf16[16,16,256]{2,1,0:T(8,128)(2,1)S(1)} %shard_map.100), channel_id=1, replica_groups=mesh['x'=4,'yh'=4,'yl'=2,'zh'=4,'zl'=2,'c'=2] {'c','zh','zl'}, dimensions={0} | all-to-all | bytes 262144 | tf_op jit(solution)/shard_map/all_to_all | solution.py:230
  149.0 0.7 copy.11
  (1 shorter events, 0.0 us)
Async XLA Ops:
  28.0 18.3 %copy-start = (s32[832,256]{1,0:T(8,128)S(1)}, s32[832,256]{1,0:T(8,128)}, u32[]{:S(2)}) copy-start(s32[832,256]{1,0:T(8,128)} %codes.1) | copy-start | bytes 2555908
  28.0 18.3 %copy-start.1 = (bf16[13,256]{1,0:T(8,128)(2,1)S(1)}, bf16[13,256]{1,0:T(8,128)(2,1)}, u32[]{:S(2)}) copy-start(bf16[13,256]{1,0:T(8,128)(2,1)} %scales.1) | copy-start | bytes 19972
  29.0 29.3 %all-to-all-start.1 = ((bf16[16,8,896]{2,1,0:T(8,128)(2,1)}), bf16[16,8,896]{2,1,0:T(8,128)(2,1)S(1)}, u32[]{:S(2)}, u32[]{:S(2)}) async-start(bf16[16,8,896]{2,1,0:T(8,128)(2,1)} %shard_map.92), calls=%async_computation.1 | async-start | bytes 458752 | tf_op jit(solution)/shard_map/all_to_all | solution.py:230
  46.8 26.6 %collective-permute-start = (bf16[1664,256]{1,0:T(8,128)(2,1)S(1)}, bf16[1664,256]{1,0:T(8,128)(2,1)S(1)}, u32[]{:S(2)}, u32[]{:S(2)}) collective-permute-start(bf16[1664,256]{1,0:T(8,128)(2,1)S(1)} %shard_map.95.own_ref), channel_id=1, source_target_pairs={{0,1},{1,0},{2,3},{3,2},{4,5},{5,4},{6,7},{7,6},{8,9},{9,8},{10,11... | collective-permute-start | bytes 2555912 | tf_op jit(solution)/shard_map/ppermute | solution.py:238
  69.9 53.6 %all-to-all-start.3 = ((bf16[8,32,1664]{2,1,0:T(8,128)(2,1)}), bf16[8,32,1664]{2,1,0:T(8,128)(2,1)S(1)}, u32[]{:S(2)}, u32[]{:S(2)}) async-start(bf16[8,32,1664]{2,1,0:T(8,128)(2,1)} %shard_map.94), calls=%async_computation.3 | async-start | bytes 1703936 | tf_op jit(solution)/shard_map/all_to_all | solution.py:230
  73.7 10.8 %collective-permute-start.1 = (bf16[416,256]{1,0:T(8,128)(2,1)S(1)}, bf16[416,256]{1,0:T(8,128)(2,1)S(1)}, u32[]{:S(2)}, u32[]{:S(2)}) collective-permute-start(bf16[416,256]{1,0:T(8,128)(2,1)S(1)} %get-tuple-element.13), channel_id=1, source_target_pairs={{0,4},{4,8},{8,12},{12,0},{1,5},{5,9},{9,13},{13,1},{2,6},{6,10},{... | collective-permute-start | bytes 638984 | tf_op jit(solution)/shard_map/ppermute | solution.py:274
  75.6 21.0 %collective-permute-start.2 = (bf16[416,256]{1,0:T(8,128)(2,1)S(1)}, bf16[416,256]{1,0:T(8,128)(2,1)S(1)}, u32[]{:S(2)}, u32[]{:S(2)}) collective-permute-start(bf16[416,256]{1,0:T(8,128)(2,1)S(1)} %get-tuple-element.14), channel_id=1, source_target_pairs={{0,8},{4,12},{8,0},{12,4},{1,9},{5,13},{9,1},{13,5},{2,10},{6,14},... | collective-permute-start | bytes 638984 | tf_op jit(solution)/shard_map/ppermute | solution.py:274
  81.3 20.7 %collective-permute-start.3 = (bf16[416,256]{1,0:T(8,128)(2,1)S(1)}, bf16[416,256]{1,0:T(8,128)(2,1)S(1)}, u32[]{:S(2)}, u32[]{:S(2)}) collective-permute-start(bf16[416,256]{1,0:T(8,128)(2,1)S(1)} %get-tuple-element.15), channel_id=1, source_target_pairs={{0,12},{4,0},{8,4},{12,8},{1,13},{5,1},{9,5},{13,9},{2,14},{6,2},{... | collective-permute-start | bytes 638984 | tf_op jit(solution)/shard_map/ppermute | solution.py:274
  102.1 21.0 %collective-permute-start.4 = (bf16[1664,256]{1,0:T(8,128)(2,1)S(1)}, bf16[1664,256]{1,0:T(8,128)(2,1)S(1)}, u32[]{:S(2)}, u32[]{:S(2)}) collective-permute-start(bf16[1664,256]{1,0:T(8,128)(2,1)S(1)} %shard_map.97.own_ref), channel_id=1, source_target_pairs={{0,2},{2,0},{1,3},{3,1},{4,6},{6,4},{5,7},{7,5},{8,10},{10,8},{9,1... | collective-permute-start | bytes 2555912 | tf_op jit(solution)/shard_map/ppermute | solution.py:238

commit v7 on v6

--- a/solution.py
+++ b/solution.py
@@ -144,7 +144,7 @@
         out_ref[pl.ds(block * FACTOR, FACTOR), :] = mixed.astype(BF16)
 
 
-def sum_near(parts, out_ref, total, joined):
+def sum_near(parts, out_hbm, total, joined, ready, sems):
     def summed(first, width):
         value = parts[0, first : first + width].astype(F32)
         for source in range(1, N_NEAR):
@@ -156,13 +156,16 @@
     tile = summed(TILES - 1, 1).reshape(8, 128)
     squares = jnp.concatenate([tile[:, 2 * i : 2 * i + 1] + tile[:, 2 * i + 1 : 2 * i + 2] for i in range(4)], axis=0)
     tail = two_parts(squares, 64)
+    leaving = []
     for piece in range(N_ZH):
         joined[:, 0:SLICE] = total[:, piece * SLICE : (piece + 1) * SLICE]
         joined[:, SLICE : 2 * SLICE] = total[:, LOCAL + piece * SLICE : LOCAL + (piece + 1) * SLICE]
         joined[:, 2 * SLICE : PIECE] = tail
-        value = joined[...].astype(BF16)
-        for yh in range(N_YH):
-            out_ref[piece * N_YH + yh] = value[8 * yh : 8 * yh + 8, :]
+        ready[piece] = joined[...].reshape(N_YH, 8, PIECE).astype(BF16)
+        leaving.append(pltpu.make_async_copy(ready.at[piece], out_hbm.at[pl.ds(piece * N_YH, N_YH)], sems.at[piece]))
+        leaving[-1].start()
+    for copy in leaving:
+        copy.wait()
 
 
 def source_of(shift):
@@ -275,7 +278,14 @@
     weight = call(join, shape((LOCAL, columns), BF16))(*dealt)
     other = swapped(weight, "zl")
     scratch = [pltpu.VMEM((NEAR_ROWS, 2 * LOCAL), F32), pltpu.VMEM((NEAR_ROWS, PIECE), F32)]
-    pieces = call(sum_near, shape((N_YH * N_ZH, 8, PIECE), BF16), scratch)(near)
+    scratch += [pltpu.VMEM((N_ZH, N_YH, 8, PIECE), BF16), pltpu.SemaphoreType.DMA((N_ZH,))]
+    pieces = pl.pallas_call(
+        sum_near,
+        out_shape=shape((N_ZH * N_YH, 8, PIECE), BF16),
+        out_specs=pl.BlockSpec(memory_space=pltpu.HBM),
+        scratch_shapes=scratch,
+        compiler_params=pltpu.CompilerParams(vmem_limit_bytes=48 << 20),
+    )(near)
     far = exchange(pieces, FAR)
     scratch = [pltpu.VMEM((8, PIECE), F32), pltpu.VMEM((N_ZH, 8, SLICE), F32), pltpu.VMEM((8, LOCAL), F32)]
     mixed = call(activate, shape((N_YH, 8, LOCAL), BF16), scratch)(far)

time: 150 us -> 150 us (level)
  no operation moved by 1% of the time
where the time goes in v7:
time: 150 us
  blocking collectives  60.2 us (40%)
  waiting for transfers between devices  43.7 us (29%)
  starting transfers between devices  37.9 us (25%)
  Pallas kernels  7.09 us (5%)
    all_to_all x4, blocking collectives, exchange(): return lax.all_to_all(blocks, axes, split_axis=0, concat_axis=0, tiled=True)  60.2 us
    all_to_all x2, starting transfers between devices, exchange(): return lax.all_to_all(blocks, axes, split_axis=0, concat_axis=0, tiled=True)  20.8 us
    ppermute x2, waiting for transfers between devices, swapped(): return lax.ppermute(weight, axis, [(0, 1), (1, 0)])  19.1 us
    ppermute x3, waiting for transfers between devices, shards(): lax.ppermute(groups[j], 'zh', [(i, (i + j) % N_ZH) for i in range(N_ZH)])  17.5 us
    ppermute x3, starting transfers between devices, shards(): lax.ppermute(groups[j], 'zh', [(i, (i + j) % N_ZH) for i in range(N_ZH)])  10.8 us
    all_to_all x2, waiting for transfers between devices, exchange(): return lax.all_to_all(blocks, axes, split_axis=0, concat_axis=0, tiled=True)  7.04 us
    ppermute x2, starting transfers between devices, swapped(): return lax.ppermute(weight, axis, [(0, 1), (1, 0)])  6.3 us
    pallas_call x1, Pallas kernels, shards(): pl.pallas_call(project_in, out_shape=[shape((N_NEAR, TILES, 8, 128), BF16...  3.2 us
  transfers between devices with their start and end apart: 7, of which 4 were waited for; matrix products, arithmetic and copies ran while one was open for 0% of the time, Pallas kernels for 2%

profile of v7, /device:TPU:1, one launch (start us, length us, event | category | flops | bytes accessed | tf_op | source)
XLA Modules:
  0.0 149.7 jit_solution(16904705236783118311)
XLA Ops:
  0.0 3.2 %shard_map.91 = (bf16[8,105,8,128]{3,2,1,0:T(8,128)(2,1)S(1)}, bf16[16,256]{1,0:T(8,128)(2,1)S(1)}) custom-call(bf16[256,256]{1,0:T(8,128)(2,1)} %x_hbm.1, bf16[256]{0:T(256)(128)(2,1)} %gain_hbm.1, s32[128,1664]{1,0:T(8,128)} %gate_hbm.1, bf16[2,1664]{1,0:T(2,128)(2,1)} %gate_scales_hbm.1, s32[128,1664]{1,0:T(8,128)} %up_hbm.1, ...), custom_call_target="tpu_custom_call" | custom-call | tf_op jit(solution)/shard_map/pallas_call | solution.py:262
  3.2 24.8 %all_to_all.30.parts = bf16[8,105,8,128]{3,2,1,0:T(8,128)(2,1)S(1)} all-to-all(bf16[8,105,8,128]{3,2,1,0:T(8,128)(2,1)S(1)} %get-tuple-element.11), channel_id=1, replica_groups=mesh['x'=4,'yh'=4,'yl'=2,'zh'=4,'zl'=2,'c'=2] {'yl','x'}, dimensions={0} | all-to-all | bytes 3440640 | tf_op jit(solution)/shard_map/all_to_all | solution.py:233
  28.0 0.0 copy-start
  28.0 0.0 copy-start.1
  28.0 1.0 shard_map.92
  29.0 17.3 %all-to-all-start.1 = ((bf16[16,8,896]{2,1,0:T(8,128)(2,1)}), bf16[16,8,896]{2,1,0:T(8,128)(2,1)S(1)}, u32[]{:S(2)}, u32[]{:S(2)}) async-start(bf16[16,8,896]{2,1,0:T(8,128)(2,1)} %shard_map.92), calls=%async_computation.1 | async-start | bytes 458752 | tf_op jit(solution)/shard_map/all_to_all | solution.py:233
  46.3 0.0 copy-done
  46.3 0.0 copy-done.1
  46.3 0.5 shard_map.95.own_ref
  46.9 4.4 %collective-permute-start = (bf16[1664,256]{1,0:T(8,128)(2,1)S(1)}, bf16[1664,256]{1,0:T(8,128)(2,1)S(1)}, u32[]{:S(2)}, u32[]{:S(2)}) collective-permute-start(bf16[1664,256]{1,0:T(8,128)(2,1)S(1)} %shard_map.95.own_ref), channel_id=1, source_target_pairs={{0,1},{1,0},{2,3},{3,2},{4,5},{5,4},{6,7},{7,6},{8,9},{9,8},{10,11... | collective-permute-start | bytes 2555912 | tf_op jit(solution)/shard_map/ppermute | solution.py:241
  51.3 7.0 %all-to-all-done.1.parts = bf16[16,8,896]{2,1,0:T(8,128)(2,1)S(1)} async-done(((bf16[16,8,896]{2,1,0:T(8,128)(2,1)}), bf16[16,8,896]{2,1,0:T(8,128)(2,1)S(1)}, u32[]{:S(2)}, u32[]{:S(2)}) %all-to-all-start.1) | async-done | bytes 229408 | tf_op jit(solution)/shard_map/all_to_all | solution.py:233
  58.3 0.3 shard_map.93
  58.6 10.3 %all_to_all.31.parts = bf16[4,8,1664]{2,1,0:T(8,128)(2,1)S(1)} all-to-all(bf16[4,8,1664]{2,1,0:T(8,128)(2,1)S(1)} %shard_map.93), channel_id=1, replica_groups=mesh['x'=4,'yh'=4,'yl'=2,'zh'=4,'zl'=2,'c'=2] {'yh'}, dimensions={0} | all-to-all | bytes 212992 | tf_op jit(solution)/shard_map/all_to_all | solution.py:233
  68.9 1.0 shard_map.94
  69.9 3.5 %all-to-all-start.3 = ((bf16[8,32,1664]{2,1,0:T(8,128)(2,1)}), bf16[8,32,1664]{2,1,0:T(8,128)(2,1)S(1)}, u32[]{:S(2)}, u32[]{:S(2)}) async-start(bf16[8,32,1664]{2,1,0:T(8,128)(2,1)} %shard_map.94), calls=%async_computation.3 | async-start | bytes 1703936 | tf_op jit(solution)/shard_map/all_to_all | solution.py:233
  73.5 0.0 collective-permute-done.other_ref
  73.5 0.3 shard_map.96
  73.7 1.9 %collective-permute-start.1 = (bf16[416,256]{1,0:T(8,128)(2,1)S(1)}, bf16[416,256]{1,0:T(8,128)(2,1)S(1)}, u32[]{:S(2)}, u32[]{:S(2)}) collective-permute-start(bf16[416,256]{1,0:T(8,128)(2,1)S(1)} %get-tuple-element.13), channel_id=1, source_target_pairs={{0,4},{4,8},{8,12},{12,0},{1,5},{5,9},{9,13},{13,1},{2,6},{6,10},{... | collective-permute-start | bytes 638984 | tf_op jit(solution)/shard_map/ppermute | solution.py:277
  75.7 5.7 %collective-permute-start.2 = (bf16[416,256]{1,0:T(8,128)(2,1)S(1)}, bf16[416,256]{1,0:T(8,128)(2,1)S(1)}, u32[]{:S(2)}, u32[]{:S(2)}) collective-permute-start(bf16[416,256]{1,0:T(8,128)(2,1)S(1)} %get-tuple-element.14), channel_id=1, source_target_pairs={{0,8},{4,12},{8,0},{12,4},{1,9},{5,13},{9,1},{13,5},{2,10},{6,14},... | collective-permute-start | bytes 638984 | tf_op jit(solution)/shard_map/ppermute | solution.py:277
  81.4 3.2 %collective-permute-start.3 = (bf16[416,256]{1,0:T(8,128)(2,1)S(1)}, bf16[416,256]{1,0:T(8,128)(2,1)S(1)}, u32[]{:S(2)}, u32[]{:S(2)}) collective-permute-start(bf16[416,256]{1,0:T(8,128)(2,1)S(1)} %get-tuple-element.15), channel_id=1, source_target_pairs={{0,12},{4,0},{8,4},{12,8},{1,13},{5,1},{9,5},{13,9},{2,14},{6,2},{... | collective-permute-start | bytes 638984 | tf_op jit(solution)/shard_map/ppermute | solution.py:277
  84.6 0.0 collective-permute-done.1.refs_1_
  84.6 12.1 %collective-permute-done.2.refs_2_ = bf16[416,256]{1,0:T(8,128)(2,1)S(1)} collective-permute-done((bf16[416,256]{1,0:T(8,128)(2,1)S(1)}, bf16[416,256]{1,0:T(8,128)(2,1)S(1)}, u32[]{:S(2)}, u32[]{:S(2)}) %collective-permute-start.2) | collective-permute-done | bytes 213024 | tf_op jit(solution)/shard_map/ppermute | solution.py:277
  96.7 5.4 %collective-permute-done.3.refs_3_ = bf16[416,256]{1,0:T(8,128)(2,1)S(1)} collective-permute-done((bf16[416,256]{1,0:T(8,128)(2,1)S(1)}, bf16[416,256]{1,0:T(8,128)(2,1)S(1)}, u32[]{:S(2)}, u32[]{:S(2)}) %collective-permute-start.3) | collective-permute-done | bytes 213024 | tf_op jit(solution)/shard_map/ppermute | solution.py:277
  102.1 0.1 shard_map.97.own_ref
  102.2 1.9 %collective-permute-start.4 = (bf16[1664,256]{1,0:T(8,128)(2,1)S(1)}, bf16[1664,256]{1,0:T(8,128)(2,1)S(1)}, u32[]{:S(2)}, u32[]{:S(2)}) collective-permute-start(bf16[1664,256]{1,0:T(8,128)(2,1)S(1)} %shard_map.97.own_ref), channel_id=1, source_target_pairs={{0,2},{2,0},{1,3},{3,1},{4,6},{6,4},{5,7},{7,5},{8,10},{10,8},{9,1... | collective-permute-start | bytes 2555912 | tf_op jit(solution)/shard_map/ppermute | solution.py:241
  104.1 19.1 %collective-permute-done.4.other_ref = bf16[1664,256]{1,0:T(8,128)(2,1)S(1)} collective-permute-done((bf16[1664,256]{1,0:T(8,128)(2,1)S(1)}, bf16[1664,256]{1,0:T(8,128)(2,1)S(1)}, u32[]{:S(2)}, u32[]{:S(2)}) %collective-permute-start.4) | collective-permute-done | bytes 852000 | tf_op jit(solution)/shard_map/ppermute | solution.py:241
  123.2 0.3 shard_map.98.weight
  123.5 0.0 all-to-all-done.3
  123.5 0.4 shard_map.99
  123.9 13.6 %all_to_all.32.parts = bf16[16,16,256]{2,1,0:T(8,128)(2,1)S(1)} all-to-all(bf16[16,16,256]{2,1,0:T(8,128)(2,1)S(1)} %bitcast.4), channel_id=1, replica_groups=mesh['x'=4,'yh'=4,'yl'=2,'zh'=4,'zl'=2,'c'=2] {'c','zh','zl'}, dimensions={0} | all-to-all | bytes 262144 | tf_op jit(solution)/shard_map/all_to_all | solution.py:233
  137.5 11.6 %all_to_all.33 = bf16[16,16,256]{2,1,0:T(8,128)(2,1)S(1)} all-to-all(bf16[16,16,256]{2,1,0:T(8,128)(2,1)S(1)} %shard_map.100), channel_id=1, replica_groups=mesh['x'=4,'yh'=4,'yl'=2,'zh'=4,'zl'=2,'c'=2] {'c','zh','zl'}, dimensions={0} | all-to-all | bytes 262144 | tf_op jit(solution)/shard_map/all_to_all | solution.py:233
  149.0 0.7 copy.11
  (1 shorter events, 0.0 us)
Async XLA Ops:
  28.0 18.3 %copy-start = (s32[832,256]{1,0:T(8,128)S(1)}, s32[832,256]{1,0:T(8,128)}, u32[]{:S(2)}) copy-start(s32[832,256]{1,0:T(8,128)} %codes.1) | copy-start | bytes 2555908
  28.0 18.3 %copy-start.1 = (bf16[13,256]{1,0:T(8,128)(2,1)S(1)}, bf16[13,256]{1,0:T(8,128)(2,1)}, u32[]{:S(2)}) copy-start(bf16[13,256]{1,0:T(8,128)(2,1)} %scales.1) | copy-start | bytes 19972
  29.0 29.3 %all-to-all-start.1 = ((bf16[16,8,896]{2,1,0:T(8,128)(2,1)}), bf16[16,8,896]{2,1,0:T(8,128)(2,1)S(1)}, u32[]{:S(2)}, u32[]{:S(2)}) async-start(bf16[16,8,896]{2,1,0:T(8,128)(2,1)} %shard_map.92), calls=%async_computation.1 | async-start | bytes 458752 | tf_op jit(solution)/shard_map/all_to_all | solution.py:233
  46.9 26.6 %collective-permute-start = (bf16[1664,256]{1,0:T(8,128)(2,1)S(1)}, bf16[1664,256]{1,0:T(8,128)(2,1)S(1)}, u32[]{:S(2)}, u32[]{:S(2)}) collective-permute-start(bf16[1664,256]{1,0:T(8,128)(2,1)S(1)} %shard_map.95.own_ref), channel_id=1, source_target_pairs={{0,1},{1,0},{2,3},{3,2},{4,5},{5,4},{6,7},{7,6},{8,9},{9,8},{10,11... | collective-permute-start | bytes 2555912 | tf_op jit(solution)/shard_map/ppermute | solution.py:241
  69.9 53.6 %all-to-all-start.3 = ((bf16[8,32,1664]{2,1,0:T(8,128)(2,1)}), bf16[8,32,1664]{2,1,0:T(8,128)(2,1)S(1)}, u32[]{:S(2)}, u32[]{:S(2)}) async-start(bf16[8,32,1664]{2,1,0:T(8,128)(2,1)} %shard_map.94), calls=%async_computation.3 | async-start | bytes 1703936 | tf_op jit(solution)/shard_map/all_to_all | solution.py:233
  73.7 10.8 %collective-permute-start.1 = (bf16[416,256]{1,0:T(8,128)(2,1)S(1)}, bf16[416,256]{1,0:T(8,128)(2,1)S(1)}, u32[]{:S(2)}, u32[]{:S(2)}) collective-permute-start(bf16[416,256]{1,0:T(8,128)(2,1)S(1)} %get-tuple-element.13), channel_id=1, source_target_pairs={{0,4},{4,8},{8,12},{12,0},{1,5},{5,9},{9,13},{13,1},{2,6},{6,10},{... | collective-permute-start | bytes 638984 | tf_op jit(solution)/shard_map/ppermute | solution.py:277
  75.7 21.0 %collective-permute-start.2 = (bf16[416,256]{1,0:T(8,128)(2,1)S(1)}, bf16[416,256]{1,0:T(8,128)(2,1)S(1)}, u32[]{:S(2)}, u32[]{:S(2)}) collective-permute-start(bf16[416,256]{1,0:T(8,128)(2,1)S(1)} %get-tuple-element.14), channel_id=1, source_target_pairs={{0,8},{4,12},{8,0},{12,4},{1,9},{5,13},{9,1},{13,5},{2,10},{6,14},... | collective-permute-start | bytes 638984 | tf_op jit(solution)/shard_map/ppermute | solution.py:277
  81.4 20.7 %collective-permute-start.3 = (bf16[416,256]{1,0:T(8,128)(2,1)S(1)}, bf16[416,256]{1,0:T(8,128)(2,1)S(1)}, u32[]{:S(2)}, u32[]{:S(2)}) collective-permute-start(bf16[416,256]{1,0:T(8,128)(2,1)S(1)} %get-tuple-element.15), channel_id=1, source_target_pairs={{0,12},{4,0},{8,4},{12,8},{1,13},{5,1},{9,5},{13,9},{2,14},{6,2},{... | collective-permute-start | bytes 638984 | tf_op jit(solution)/shard_map/ppermute | solution.py:277
  102.2 21.0 %collective-permute-start.4 = (bf16[1664,256]{1,0:T(8,128)(2,1)S(1)}, bf16[1664,256]{1,0:T(8,128)(2,1)S(1)}, u32[]{:S(2)}, u32[]{:S(2)}) collective-permute-start(bf16[1664,256]{1,0:T(8,128)(2,1)S(1)} %shard_map.97.own_ref), channel_id=1, source_target_pairs={{0,2},{2,0},{1,3},{3,1},{4,6},{6,4},{5,7},{7,5},{8,10},{10,8},{9,1... | collective-permute-start | bytes 2555912 | tf_op jit(solution)/shard_map/ppermute | solution.py:241
